TPU v7x, 32 devices: a whole 2x2x4 slice. The times are simulated.
32 devices in a mesh: fsdp: 4 (over y, core), ctx: 2 (over x), tp: 4 (over z).
Axes of the slice: x: 2, y: 2, z: 4, core: 2. Of those that a mesh axis runs over, the one named last changes fastest.
Arguments:
- block_input: bfloat16 [4096, 768], P(('fsdp', 'ctx', 'tp')), may hold values from -6 to 6
- cotangent: bfloat16 [4096, 768], P(('fsdp', 'ctx', 'tp'))
- norm1_gain: bfloat16 [768], replicated, may hold values from 0.25 to 1.75
- norm1_bias: bfloat16 [768], replicated, may hold values from -1.796875 to 1.796875
- norm2_gain: bfloat16 [768], replicated, may hold values from 0.25 to 1.75
- norm2_bias: bfloat16 [768], replicated, may hold values from -1.796875 to 1.796875
- qkv_weight: bfloat16 [3, 768, 768], P(None, ('fsdp', 'ctx'), 'tp')
- qkv_bias: bfloat16 [3, 768], P(None, 'tp'), may hold values from -3 to 3
- out_weight: bfloat16 [768, 768], P('tp', ('fsdp', 'ctx')), may hold values from -0.875 to 0.875
- out_bias: bfloat16 [768], replicated, may hold values from -1.796875 to 1.796875
- up_weight: bfloat16 [768, 3072], P(('fsdp', 'ctx'), 'tp'), may hold values from -0.21875 to 0.21875
- up_bias: bfloat16 [3072], P('tp'), may hold values from -3 to 3
- down_weight: bfloat16 [3072, 768], P('tp', ('fsdp', 'ctx')), may hold values from -0.109375 to 0.109375
- down_bias: bfloat16 [768], replicated, may hold values from -1.796875 to 1.796875
- doc_ids: int32 [4096], P(('fsdp', 'ctx')), may hold values from 0 to 7, as said below
- doc_start: int32 [4096], P(('fsdp', 'ctx')), may hold values from 0 to 1023, as said below
Outputs:
- block_output: bfloat16 [4096, 768], P(('fsdp', 'ctx', 'tp'))
- grad_input: bfloat16 [4096, 768], P(('fsdp', 'ctx', 'tp'))
- grad_qkv_weight: float32 [3, 768, 768], P(None, ('fsdp', 'ctx'), 'tp')
- grad_qkv_bias: float32 [3, 768], P(None, 'tp')
- grad_out_weight: float32 [768, 768], P('tp', ('fsdp', 'ctx'))
- grad_out_bias: float32 [768], replicated
- grad_up_weight: float32 [768, 3072], P(('fsdp', 'ctx'), 'tp')
- grad_up_bias: float32 [3072], P('tp')
- grad_down_weight: float32 [3072, 768], P('tp', ('fsdp', 'ctx'))
- grad_down_bias: float32 [768], replicated
- grad_norm1_gain: float32 [768], replicated
- grad_norm1_bias: float32 [768], replicated
- grad_norm2_gain: float32 [768], replicated
- grad_norm2_bias: float32 [768], replicated
Inputs may be any that keep to these rules, and one draw needn't show every extreme that they name: `doc_ids`: numbers the documents of each sequence of 1024 tokens from 0 at the sequence's first token; within a sequence it never falls and rises by one at the first token of each document; a sequence holds at most 8 documents. `doc_start`: the position within its sequence of the first token of the token's document: 0 at each sequence's first token, a token's own position where its document begins, equal for all tokens of one document.
All inputs are finite; a program needn't handle non-finite values.
Results may differ from a plain program's by a relative error of at most 0.009.
Values may be sent and summed in bfloat16 or wider, within the bound.
A program may use at most 128 MiB of HBM per device.

v0:
```python
import jax
import jax.numpy as jnp
from jax import lax
from jax.sharding import PartitionSpec as P

HD = 64
ROT = 16


EPS = 1e-05


def gelu_parts(pre_act):
    cumulative = 0.5 * (1.0 + jax.scipy.special.erf(pre_act * 0.7071067811865476))
    density = jnp.exp(-0.5 * pre_act * pre_act) * 0.3989422804014327
    return (pre_act * cumulative, cumulative + pre_act * density)


def angle_tables(offsets):
    half_rot = ROT // 2
    frequency = 10000.0 ** (-(2.0 * jnp.arange(half_rot, dtype=jnp.float32)) / ROT)
    angles = offsets.astype(jnp.float32)[:, None] * frequency[None, :]
    angles = jnp.concatenate([angles, angles], axis=1)
    return (jnp.cos(angles), jnp.sin(angles))


def rotate(tensor, cosine, sine_table):
    half_rot = ROT // 2
    turned = jnp.concatenate([-tensor[..., half_rot:ROT], tensor[..., :half_rot]], axis=-1)
    leading = tensor[..., :ROT] * cosine[:, None, :] + turned * sine_table[:, None, :]
    return jnp.concatenate([leading, tensor[..., ROT:]], axis=-1)


def normalize(rows_in):
    centered = rows_in - jnp.mean(rows_in, axis=1, keepdims=True)
    inv_std = lax.rsqrt(jnp.mean(centered * centered, axis=1, keepdims=True) + EPS)
    return (centered * inv_std, inv_std)


def attention_probs(queries, keys_all, query_pos, query_doc, key_doc):
    score_scale = HD ** (-0.5)
    scores = (
        jnp.einsum("qhd,khd->hqk", queries, keys_all, preferred_element_type=jnp.float32)
        * score_scale
    )
    key_pos = jnp.arange(keys_all.shape[0], dtype=jnp.int32)
    allowed = (query_doc[:, None] == key_doc[None, :]) & (key_pos[None, :] <= query_pos[:, None])
    masked = jnp.where(allowed[None], scores, -1e30)
    row_peak = jnp.max(masked, axis=2, keepdims=True)
    exponent = jnp.where(allowed[None], jnp.exp(masked - row_peak), 0.0)
    return exponent / jnp.sum(exponent, axis=2, keepdims=True)


def local(
    block_input,
    cotangent,
    norm1_gain,
    norm1_bias,
    norm2_gain,
    norm2_bias,
    qkv_weight,
    qkv_bias,
    out_weight,
    out_bias,
    up_weight,
    up_bias,
    down_weight,
    down_bias,
    doc_ids,
    doc_start,
):
    own_count = block_input.shape[0]
    local_width = qkv_weight.shape[2]
    heads_here = local_width // HD
    score_scale = HD ** (-0.5)
    full_in, full_cot = (
        lax.all_gather(block_input, "tp", axis=0, tiled=True),
        lax.all_gather(cotangent, "tp", axis=0, tiled=True),
    )
    row_count = full_in.shape[0]
    qkv_full, out_full, up_full, down_full = (
        lax.all_gather(qkv_weight, ("fsdp", "ctx"), axis=1, tiled=True),
        lax.all_gather(out_weight, ("fsdp", "ctx"), axis=1, tiled=True),
        lax.all_gather(up_weight, ("fsdp", "ctx"), axis=0, tiled=True),
        lax.all_gather(down_weight, ("fsdp", "ctx"), axis=1, tiled=True),
    )
    gain_one = norm1_gain.astype(jnp.float32)
    gain_two = norm2_gain.astype(jnp.float32)
    normed, inv_std = normalize(full_in.astype(jnp.float32))
    first_in = (normed * gain_one + norm1_bias.astype(jnp.float32)).astype(jnp.bfloat16)
    second_in = (normed * gain_two + norm2_bias.astype(jnp.float32)).astype(jnp.bfloat16)
    projected = jnp.einsum("nd,jde->jne", first_in, qkv_full, preferred_element_type=jnp.float32)
    projected = projected + qkv_bias.astype(jnp.float32)[:, None, :]
    query_pos = lax.axis_index("ctx") * row_count + jnp.arange(row_count, dtype=jnp.int32)
    cosine, sine_table = angle_tables(query_pos - doc_start)
    queries = rotate(projected[0].reshape(row_count, heads_here, HD), cosine, sine_table).astype(
        jnp.bfloat16
    )
    keys_here = rotate(projected[1].reshape(row_count, heads_here, HD), cosine, sine_table).astype(
        jnp.bfloat16
    )
    values_here = projected[2].astype(jnp.bfloat16)
    keys_flat, values_flat, key_doc = (
        lax.all_gather(keys_here.reshape(row_count, local_width), "ctx", axis=0, tiled=True),
        lax.all_gather(values_here, "ctx", axis=0, tiled=True),
        lax.all_gather(doc_ids, "ctx", axis=0, tiled=True),
    )
    length = keys_flat.shape[0]
    keys_all = keys_flat.reshape(length, heads_here, HD)
    values_all = values_flat.reshape(length, heads_here, HD)
    attn_probs = attention_probs(queries, keys_all, query_pos, doc_ids, key_doc)
    probs_b = attn_probs.astype(jnp.bfloat16)
    attended = jnp.einsum("hqk,khd->qhd", probs_b, values_all, preferred_element_type=jnp.float32)
    attended = attended.reshape(row_count, local_width).astype(jnp.bfloat16)
    pre_act = jnp.dot(second_in, up_full, preferred_element_type=jnp.float32) + up_bias.astype(
        jnp.float32
    )
    activated, gelu_slope = gelu_parts(pre_act)
    act_b = activated.astype(jnp.bfloat16)
    attn_part = jnp.dot(attended, out_full, preferred_element_type=jnp.float32)
    mlp_part = jnp.dot(act_b, down_full, preferred_element_type=jnp.float32)
    summed = lax.psum_scatter(attn_part, "tp", scatter_dimension=0, tiled=True) + lax.psum_scatter(
        mlp_part.astype(jnp.bfloat16), "tp", scatter_dimension=0, tiled=True
    ).astype(jnp.float32)
    block_output = (
        block_input.astype(jnp.float32)
        + summed
        + out_bias.astype(jnp.float32)
        + down_bias.astype(jnp.float32)
    ).astype(jnp.bfloat16)
    cot_float = cotangent.astype(jnp.float32)
    bias_grad = jnp.sum(cot_float, axis=0)
    grad_out_local = jnp.dot(attended.T, full_cot, preferred_element_type=jnp.float32)
    grad_down_local = jnp.dot(act_b.T, full_cot, preferred_element_type=jnp.float32)
    d_attended = jnp.dot(full_cot, out_full.T, preferred_element_type=jnp.float32).astype(
        jnp.bfloat16
    )
    d_pre = (
        jnp.dot(full_cot, down_full.T, preferred_element_type=jnp.float32) * gelu_slope
    ).astype(jnp.bfloat16)
    grad_up_local = jnp.dot(second_in.T, d_pre, preferred_element_type=jnp.float32)
    up_bias_grad = jnp.sum(d_pre.astype(jnp.float32), axis=0)
    d_second = jnp.dot(d_pre, up_full.T, preferred_element_type=jnp.float32)
    d_heads = d_attended.reshape(row_count, heads_here, HD)
    d_values = jnp.einsum("hqk,qhd->khd", probs_b, d_heads, preferred_element_type=jnp.float32)
    d_probs = jnp.einsum("qhd,khd->hqk", d_heads, values_all, preferred_element_type=jnp.float32)
    delta_sum = jnp.sum(attn_probs * d_probs, axis=2, keepdims=True)
    d_scores = (attn_probs * (d_probs - delta_sum)).astype(jnp.bfloat16)
    d_query = (
        jnp.einsum("hqk,khd->qhd", d_scores, keys_all, preferred_element_type=jnp.float32)
        * score_scale
    )
    d_keys = (
        jnp.einsum("hqk,qhd->khd", d_scores, queries, preferred_element_type=jnp.float32)
        * score_scale
    )
    key_grad, value_grad = (
        lax.psum_scatter(
            d_keys.reshape(length, local_width), "ctx", scatter_dimension=0, tiled=True
        ),
        lax.psum_scatter(
            d_values.reshape(length, local_width), "ctx", scatter_dimension=0, tiled=True
        ),
    )
    d_qkv = jnp.stack(
        [
            rotate(d_query, cosine, -sine_table).reshape(row_count, local_width),
            rotate(key_grad.reshape(row_count, heads_here, HD), cosine, -sine_table).reshape(
                row_count, local_width
            ),
            value_grad,
        ]
    ).astype(jnp.bfloat16)
    qkv_bias_grad = jnp.sum(d_qkv.astype(jnp.float32), axis=1)
    grad_qkv_local = jnp.einsum("nd,jne->jde", first_in, d_qkv, preferred_element_type=jnp.float32)
    d_first = jnp.einsum("jne,jde->nd", d_qkv, qkv_full, preferred_element_type=jnp.float32)
    own_start = lax.axis_index("tp") * own_count
    normed_own = lax.dynamic_slice_in_dim(normed, own_start, own_count, 0)
    inv_own = lax.dynamic_slice_in_dim(inv_std, own_start, own_count, 0)
    first_all, second_all = lax.psum((d_first, d_second), "tp")
    first_own = lax.dynamic_slice_in_dim(first_all, own_start, own_count, 0)
    second_own = lax.dynamic_slice_in_dim(second_all, own_start, own_count, 0)
    combined = first_own * gain_one + second_own * gain_two
    mean_one = jnp.mean(combined, axis=1, keepdims=True)
    mean_two = jnp.mean(combined * normed_own, axis=1, keepdims=True)
    grad_input = (cot_float + inv_own * (combined - mean_one - normed_own * mean_two)).astype(
        jnp.bfloat16
    )
    grad_qkv_w, grad_out_w, grad_up_w, grad_down_w = (
        lax.psum_scatter(grad_qkv_local, ("fsdp", "ctx"), scatter_dimension=1, tiled=True),
        lax.psum_scatter(grad_out_local, ("fsdp", "ctx"), scatter_dimension=1, tiled=True),
        lax.psum_scatter(grad_up_local, ("fsdp", "ctx"), scatter_dimension=0, tiled=True),
        lax.psum_scatter(grad_down_local, ("fsdp", "ctx"), scatter_dimension=1, tiled=True),
    )
    grad_qkv_b, grad_up_b = lax.psum((qkv_bias_grad, up_bias_grad), ("fsdp", "ctx"))
    grad_out_b, gain_one_grad, bias_one_grad, gain_two_grad, bias_two_grad = lax.psum(
        (
            bias_grad,
            jnp.sum(first_own * normed_own, axis=0),
            jnp.sum(first_own, axis=0),
            jnp.sum(second_own * normed_own, axis=0),
            jnp.sum(second_own, axis=0),
        ),
        ("fsdp", "ctx", "tp"),
    )
    return (
        block_output,
        grad_input,
        grad_qkv_w,
        grad_qkv_b,
        grad_out_w,
        grad_out_b,
        grad_up_w,
        grad_up_b,
        grad_down_w,
        grad_out_b,
        gain_one_grad,
        bias_one_grad,
        gain_two_grad,
        bias_two_grad,
    )


def solution(mesh):
    in_specs = (
        P(("fsdp", "ctx", "tp"), None),
        P(("fsdp", "ctx", "tp"), None),
        P(),
        P(),
        P(),
        P(),
        P(None, ("fsdp", "ctx"), "tp"),
        P(None, "tp"),
        P("tp", ("fsdp", "ctx")),
        P(),
        P(("fsdp", "ctx"), "tp"),
        P("tp"),
        P("tp", ("fsdp", "ctx")),
        P(),
        P(("fsdp", "ctx")),
        P(("fsdp", "ctx")),
    )
    out_specs = (
        P(("fsdp", "ctx", "tp"), None),
        P(("fsdp", "ctx", "tp"), None),
        P(None, ("fsdp", "ctx"), "tp"),
        P(None, "tp"),
        P("tp", ("fsdp", "ctx")),
        P(),
        P(("fsdp", "ctx"), "tp"),
        P("tp"),
        P("tp", ("fsdp", "ctx")),
        P(),
        P(),
        P(),
        P(),
        P(),
    )
    return jax.shard_map(local, mesh=mesh, in_specs=in_specs, out_specs=out_specs, check_vma=False)
```

profile of v0, /device:TPU:0, one launch (start us, length us, event | category | flops | bytes accessed | tf_op | source)
XLA Modules:
  0.0 530.6 jit_solution(1668127374639163485)
XLA Ops:
  9.6 21.5 %all_gather.27 = bf16[512,768]{1,0:T(8,128)(2,1)S(1)} all-gather(bf16[128,768]{1,0:T(8,128)(2,1)} %param.16), channel_id=1, replica_groups=mesh['fsdp'=4,'ctx'=2,'tp'=4] {'tp'}, dimensions={0}, use_global_device_ids=true | all-gather | bytes 983040 | tf_op jit(solution)/shard_map/all_gather | solution.py:77
  31.8 24.7 %all_gather.28 = bf16[3,768,192]{2,0,1:T(4,128)(2,1)S(1)} all-gather(bf16[3,96,192]{2,0,1:T(4,128)(2,1)S(1)} %copy.33), channel_id=1, replica_groups=mesh['fsdp'=4,'ctx'=2,'tp'=4] {'fsdp','ctx'}, dimensions={1}, use_global_device_ids=true | all-gather | bytes 995328 | tf_op jit(solution)/shard_map/all_gather | solution.py:82
  60.7 8.3 %all_gather.31 = bf16[1024,192]{0,1:T(8,128)(2,1)S(1)} all-gather(bf16[512,192]{0,1:T(8,128)(2,1)S(1)} %bitcast.94), channel_id=1, replica_groups=mesh['fsdp'=4,'ctx'=2,'tp'=4] {'ctx'}, dimensions={0}, use_global_device_ids=true | all-gather | bytes 589824 | tf_op jit(solution)/shard_map/all_gather | solution.py:104
  69.0 4.4 all-gather.1
  73.3 6.3 %all-gather = bf16[1,1024,192]{1,2,0:T(8,128)(2,1)S(1)} all-gather(bf16[1,512,192]{1,2,0:T(8,128)(2,1)S(1)} %slice.129), channel_id=2, replica_groups=mesh['fsdp'=4,'ctx'=2,'tp'=4] {'ctx'}, dimensions={1}, use_global_device_ids=true | all-gather | bytes 589824 | tf_op jit(solution)/shard_map/all_gather | solution.py:105
  79.7 18.7 %all_gather.35 = bf16[512,768]{1,0:T(8,128)(2,1)S(1)} all-gather(bf16[128,768]{1,0:T(8,128)(2,1)S(1)} %copy-done.13), channel_id=1, replica_groups=mesh['fsdp'=4,'ctx'=2,'tp'=4] {'tp'}, dimensions={0}, use_global_device_ids=true | all-gather | bytes 983040 | tf_op jit(solution)/shard_map/all_gather | solution.py:78
  98.5 15.9 %all_gather.32 = bf16[192,768]{0,1:T(8,128)(2,1)S(1)} all-gather(bf16[192,96]{0,1:T(8,128)(2,1)S(1)} %copy.35), channel_id=1, replica_groups=mesh['fsdp'=4,'ctx'=2,'tp'=4] {'fsdp','ctx'}, dimensions={1}, use_global_device_ids=true | all-gather | bytes 331776 | tf_op jit(solution)/shard_map/all_gather | solution.py:83
  115.5 5.5 %fusion.53 = (f32[3,512]{1,0:T(4,128)S(1)}, f32[3,512,1024]{2,1,0:T(8,128)}) fusion(pred[512,1024]{1,0:T(8,128)(4,1)S(1)} %fusion.7, bf16[1024,3,64]{0,2,1:T(8,128)(2,1)S(1)} %bitcast.75, bf16[512,3,48]{0,2,1:T(8,128)(2,1)S(1)} %slice.133, bf16[512,3,16]{0,2,1:T(8,128)(2,1)S(1)} %get-tuple-element.72), kind=kOutput, calls=%fused_computation.109 | convolution fusion | flops 209585152 | bytes 7411712 | tf_op jit(solution)/shard_map/sub | solution.py:50
  121.0 3.7 multiply_reduce_fusion
  128.4 4.5 fusion.17
  133.0 4.3 fusion.22
  144.3 3.9 multiply_convert_fusion.1
  148.2 3.3 convolution_convert_fusion
  156.4 8.4 %reduce-scatter.19.cloned.1.call-done = f32[512,192]{0,1:T(8,128)} async-done(((f32[1024,192]{0,1:T(8,128)}), f32[512,192]{0,1:T(8,128)}) %reduce-scatter.19.cloned.1.call-update) | async-done | bytes 393232 | tf_op jit(solution)/shard_map/reduce_scatter | solution.py:161
  168.6 2.9 copy.38
  188.9 13.9 %reduce-scatter.27.cloned.1.call-done = f32[96,192]{1,0:T(8,128)} async-done(((f32[768,192]{1,0:T(8,128)}), f32[96,192]{1,0:T(8,128)}) %reduce-scatter.27.cloned.1.call-update) | async-done | bytes 73744
  204.6 14.3 %all-reduce.1 = (f32[3,192]{1,0:T(4,128)}, f32[768]{0:T(1024)}) all-reduce(f32[3,192]{1,0:T(4,128)S(1)} %convert_reduce_fusion.2, f32[768]{0:T(1024)S(1)} %get-tuple-element.83), channel_id=1, replica_groups=mesh['fsdp'=4,'ctx'=2,'tp'=4] {'fsdp','ctx'}, use_global_device_ids=true, to_apply=%region_15.16 | all-reduce | flops 1344 | bytes 10752 | tf_op jit(solution)/shard_map/psum | solution.py:195
  218.9 21.6 %reduce-scatter.13.cloned.1.call-done = f32[128,768]{1,0:T(8,128)} async-done(((f32[512,768]{1,0:T(8,128)}), f32[128,768]{1,0:T(8,128)}) %reduce-scatter.13.cloned.1.call-update) | async-done | bytes 393232 | tf_op jit(solution)/shard_map/reduce_scatter | solution.py:122
  240.6 24.4 %reduce-scatter.15.cloned.1.call-done = bf16[128,768]{1,0:T(8,128)(2,1)} async-done(((bf16[512,768]{1,0:T(8,128)(2,1)}), bf16[128,768]{1,0:T(8,128)(2,1)}) %reduce-scatter.15.cloned.1.call-update) | async-done | bytes 196624 | tf_op jit(solution)/shard_map/reduce_scatter | solution.py:122
  266.8 41.1 %reduce-scatter.25.cloned.1.call-done = f32[96,576]{1,0:T(8,128)} async-done(((f32[768,576]{1,0:T(8,128)}), f32[96,576]{1,0:T(8,128)}) %reduce-scatter.25.cloned.1.call-update) | async-done | bytes 221200
  309.7 121.3 %all-reduce.5.cloned.1.call-done = (f32[512,768]{1,0:T(8,128)}, f32[512,768]{1,0:T(8,128)}) async-done(((f32[512,768]{1,0:T(8,128)}, f32[512,768]{1,0:T(8,128)}), (f32[512,768]{1,0:T(8,128)}, f32[512,768]{1,0:T(8,128)})) %all-reduce.5.cloned.1.call-update) | async-done | bytes 3145744 | tf_op jit(solution)/shard_map/psum | solution.py:180
  433.3 39.7 %all-reduce = (f32[768]{0:T(1024)S(1)}, f32[768]{0:T(1024)}, f32[768]{0:T(1024)}, f32[768]{0:T(1024)}, f32[768]{0:T(1024)}) all-reduce(f32[768]{0:T(1024)S(1)} %get-tuple-element.68, f32[768]{0:T(1024)S(1)} %get-tuple-element.45, f32[768]{0:T(1024)S(1)} %get-tuple-element.46, ...), channel_id=1, replica_groups=mesh['fsdp'=4,'ctx'=2,'tp'=4] {'fsdp','ctx','tp'}, use_global_device_ids=true, to_apply=%region_18.19 | all-reduce | flops 3840 | bytes 30720 | tf_op jit(solution)/shard_map/psum | solution.py:196
  473.0 3.2 reduce-scatter.21.cloned.1.call-done
  476.2 46.2 %reduce-scatter.23.cloned.1.call-done = f32[768,96]{0,1:T(8,128)} async-done(((f32[768,768]{0,1:T(8,128)}), f32[768,96]{0,1:T(8,128)}) %reduce-scatter.23.cloned.1.call-update) | async-done | bytes 294928 | tf_op jit(solution)/shard_map/reduce_scatter | solution.py:193
  (181 shorter events, 52.0 us)
Async XLA Ops:
  8.0 23.7 %copy-start.35 = (bf16[768]{0:T(1024)(128)(2,1)S(1)}, bf16[768]{0:T(1024)(128)(2,1)}, u32[]{:S(2)}) copy-start(bf16[768]{0:T(1024)(128)(2,1)} %param.18) | copy-start | bytes 4612
  8.0 23.7 %copy-start.25 = (bf16[3,96,192]{2,1,0:T(8,128)(2,1)S(1)}, bf16[3,96,192]{2,1,0:T(8,128)(2,1)}, u32[]{:S(2)}) copy-start(bf16[3,96,192]{2,1,0:T(8,128)(2,1)} %param.22) | copy-start | bytes 331780
  8.0 136.3 %all-gather.5.cloned.1.call-start = ((), (), s32[]{:S(2)}) async-start(), calls=%async_computation.9 | async-start | bytes 1327104 | tf_op jit(solution)/shard_map/all_gather | solution.py:84
  8.8 139.5 %all-gather.7.cloned.1.call-start = ((), (), s32[]{:S(2)}) async-start(), calls=%async_computation.10 | async-start | bytes 1327104 | tf_op jit(solution)/shard_map/all_gather | solution.py:85
  9.5 144.0 %reduce-scatter.17.cloned.1.call-start = ((), (), s32[]{:S(2)}) async-start(), calls=%async_computation.12 | async-start | bytes 1179648 | tf_op jit(solution)/shard_map/reduce_scatter | solution.py:158
  31.1 26.4 %copy-start = (bf16[512,768]{1,0:T(8,128)(2,1)}, bf16[512,768]{1,0:T(8,128)(2,1)S(1)}, u32[]{:S(2)}) copy-start(bf16[512,768]{1,0:T(8,128)(2,1)S(1)} %all_gather.27) | copy-start | bytes 2359300
  31.7 25.8 %copy-start.28 = (f32[512]{0:T(512)}, f32[512]{0:T(512)S(1)}, u32[]{:S(2)}) copy-start(f32[512]{0:T(512)S(1)} %add_rsqrt_fusion) | copy-start | bytes 6148
  58.8 56.7 %copy-start.18 = (bf16[512,3,48]{0,2,1:T(8,128)(2,1)}, bf16[512,3,48]{0,2,1:T(8,128)(2,1)S(1)}, u32[]{:S(2)}) copy-start(bf16[512,3,48]{0,2,1:T(8,128)(2,1)S(1)} %slice.133) | copy-start | bytes 442372
  60.1 38.4 %copy-start.26 = (bf16[192,96]{1,0:T(8,128)(2,1)S(1)}, bf16[192,96]{1,0:T(8,128)(2,1)}, u32[]{:S(2)}) copy-start(bf16[192,96]{1,0:T(8,128)(2,1)} %param.24) | copy-start | bytes 110596
  60.1 55.4 %copy-start.22 = (bf16[512,3,16]{0,2,1:T(8,128)(2,1)}, bf16[512,3,16]{0,2,1:T(8,128)(2,1)S(1)}, u32[]{:S(2)}) copy-start(bf16[512,3,16]{0,2,1:T(8,128)(2,1)S(1)} %get-tuple-element.72) | copy-start | bytes 147460
  69.0 46.5 %copy-start.7 = (bf16[1024,192]{0,1:T(8,128)(2,1)}, bf16[1024,192]{0,1:T(8,128)(2,1)S(1)}, u32[]{:S(2)}) copy-start(bf16[1024,192]{0,1:T(8,128)(2,1)S(1)} %all_gather.31) | copy-start | bytes 1179652
  79.7 41.3 %copy-start.20 = (bf16[1,1024,192]{1,2,0:T(8,128)(2,1)}, bf16[1,1024,192]{1,2,0:T(8,128)(2,1)S(1)}, u32[]{:S(2)}) copy-start(bf16[1,1024,192]{1,2,0:T(8,128)(2,1)S(1)} %all-gather) | copy-start | bytes 1179652
  98.4 22.6 %copy-start.3 = (bf16[512,768]{1,0:T(8,128)(2,1)}, bf16[512,768]{1,0:T(8,128)(2,1)S(1)}, u32[]{:S(2)}) copy-start(bf16[512,768]{1,0:T(8,128)(2,1)S(1)} %all_gather.35) | copy-start | bytes 2359300
  128.4 36.4 %reduce-scatter.19.cloned.1.call-start = ((), (), s32[]{:S(2)}) async-start(), calls=%async_computation.13 | async-start | bytes 1179648 | tf_op jit(solution)/shard_map/reduce_scatter | solution.py:161
  133.0 69.8 %reduce-scatter.27.cloned.1.call-start = ((), (), s32[]{:S(2)}) async-start(), calls=%async_computation.17 | async-start | bytes 884736
  139.4 101.2 %reduce-scatter.13.cloned.1.call-start = ((), (), s32[]{:S(2)}) async-start(), calls=%async_computation.8 | async-start | bytes 1966080 | tf_op jit(solution)/shard_map/reduce_scatter | solution.py:122
  142.0 123.0 %reduce-scatter.15.cloned.1.call-start = ((), (), s32[]{:S(2)}) async-start(), calls=%async_computation.11 | async-start | bytes 983040 | tf_op jit(solution)/shard_map/reduce_scatter | solution.py:122
  151.5 156.3 %reduce-scatter.25.cloned.1.call-start = ((), (), s32[]{:S(2)}) async-start(), calls=%async_computation.16 | async-start | bytes 2211840
  174.4 256.6 %all-reduce.5.cloned.1.call-start = ((), (), s32[]{:S(2)}) async-start(), calls=%async_computation.18 | async-start | bytes 6291456 | tf_op jit(solution)/shard_map/psum | solution.py:180
  180.9 295.2 %reduce-scatter.21.cloned.1.call-start = ((), (), s32[]{:S(2)}) async-start(), calls=%async_computation.14 | async-start | bytes 2654208 | tf_op jit(solution)/shard_map/reduce_scatter | solution.py:192
  184.5 337.8 %reduce-scatter.23.cloned.1.call-start = ((), (), s32[]{:S(2)}) async-start(), calls=%async_computation.15 | async-start | bytes 2654208 | tf_op jit(solution)/shard_map/reduce_scatter | solution.py:193
  188.6 76.4 %copy-start.17 = (bf16[128,768]{1,0:T(8,128)(2,1)S(1)}, bf16[128,768]{1,0:T(8,128)(2,1)}, u32[]{:S(2)}) copy-start(bf16[128,768]{1,0:T(8,128)(2,1)} %param.16) | copy-start | bytes 589828
  266.8 165.7 %copy-start.14 = (bf16[128,768]{1,0:T(8,128)(2,1)S(1)}, bf16[128,768]{1,0:T(8,128)(2,1)}, u32[]{:S(2)}) copy-start(bf16[128,768]{1,0:T(8,128)(2,1)} %param.17) | copy-start | bytes 589828
  473.0 50.0 %copy-start.34 = (f32[768]{0:T(1024)}, f32[768]{0:T(1024)S(1)}, u32[]{:S(2)}) copy-start(f32[768]{0:T(1024)S(1)} %get-tuple-element.110) | copy-start | bytes 9220
  (33 other events, 116.1 us)
Sparse Core Ops, SparseCore 0:
  10.7 26.6 all-gather.4
  39.3 27.4 all-gather.6
Sparse Core Ops, SparseCore 1:
  128.5 16.7 reduce-scatter.16
  147.3 17.4 reduce-scatter.18
  167.8 34.9 reduce-scatter.26
  205.1 35.4 reduce-scatter.12
  242.9 22.0 reduce-scatter.14
  268.4 39.4 reduce-scatter.24
  310.1 120.9 all-reduce.4
  434.8 41.3 reduce-scatter.20
  480.0 42.3 reduce-scatter.22
where the time goes:
time: 532 us; the launch traced here: 531 us
  waiting for transfers between devices  282 us (53%)
  blocking collectives  154 us (29%)
  matrix products  44.9 us (8%)
  local copies, waits for them, and re-layouts  20.4 us (4%)
  between operations  16.4 us (3%)
  other arithmetic  12.6 us (2%)
    psum x1, waiting for transfers between devices, local(): first_all, second_all = lax.psum((d_first, d_second), 'tp')  121 us
    unnamed x13, waiting for transfers between devices  56.5 us
    reduce_scatter x1, waiting for transfers between devices, local(): lax.psum_scatter(grad_down_local, ('fsdp', 'ctx'), scatter_dimension=1, t...  46.2 us
    psum x1, blocking collectives, local(): lax.psum((bias_grad, jnp.sum(first_own * normed_own, axis=0), jnp.sum(fir...  39.7 us
    all_gather x1, blocking collectives, local(): lax.all_gather(qkv_weight, ('fsdp', 'ctx'), axis=1, tiled=True)  24.7 us
    reduce_scatter x1, waiting for transfers between devices, local(): lax.psum_scatter(mlp_part.astype(jnp.bfloat16), 'tp', scatter_dimension=0...  24.4 us
    reduce_scatter x1, waiting for transfers between devices, local(): lax.psum_scatter(attn_part, 'tp', scatter_dimension=0, tiled=True)  21.6 us
    all_gather x1, blocking collectives, local(): lax.all_gather(block_input, 'tp', axis=0, tiled=True)  21.5 us
  transfers between devices with their start and end apart: 11, of which 8 were waited for; matrix products, arithmetic and copies ran while one was open for 13% of the time, Pallas kernels for 0%

commit v1 on v0

v1 whole, which is shorter than its diff:
```python
import jax
import jax.numpy as jnp
from jax import lax
from jax.experimental import pallas as pl
from jax.experimental.pallas import tpu as pltpu
import functools
from jax.sharding import PartitionSpec as P

HD = 64
ROT = 16


EPS = 1e-05


def gelu_parts(pre_act):
    cumulative = 0.5 * (1.0 + jax.scipy.special.erf(pre_act * 0.7071067811865476))
    density = jnp.exp(-0.5 * pre_act * pre_act) * 0.3989422804014327
    return (pre_act * cumulative, cumulative + pre_act * density)


def angle_tables(offsets):
    half_rot = ROT // 2
    frequency = 10000.0 ** (-(2.0 * jnp.arange(half_rot, dtype=jnp.float32)) / ROT)
    angles = offsets.astype(jnp.float32)[:, None] * frequency[None, :]
    angles = jnp.concatenate([angles, angles], axis=1)
    return (jnp.cos(angles), jnp.sin(angles))


def rotate(tensor, cosine, sine_table):
    half_rot = ROT // 2
    turned = jnp.concatenate([-tensor[..., half_rot:ROT], tensor[..., :half_rot]], axis=-1)
    leading = tensor[..., :ROT] * cosine[:, None, :] + turned * sine_table[:, None, :]
    return jnp.concatenate([leading, tensor[..., ROT:]], axis=-1)


def normalize(rows_in):
    centered = rows_in - jnp.mean(rows_in, axis=1, keepdims=True)
    inv_std = lax.rsqrt(jnp.mean(centered * centered, axis=1, keepdims=True) + EPS)
    return (centered * inv_std, inv_std)


MESH = pl.DeviceIdType.MESH
VMEM = pl.BlockSpec(memory_space=pltpu.VMEM)
ANY = pl.BlockSpec(memory_space=pl.ANY)
PLANE = ("fsdp", "ctx")


def position():
    f = lax.axis_index("fsdp")
    return lax.rem(f, 2), f // 2, lax.axis_index("ctx"), lax.axis_index("tp")


def partner():
    core, y, _, _ = position()
    return {"fsdp": y * 2 + 1 - core}


def x_peer():
    return {"ctx": 1 - lax.axis_index("ctx")}


def y_peer():
    core, y, _, _ = position()
    return {"fsdp": (1 - y) * 2 + core}


def plane_peer(step):
    rank = lax.rem(lax.axis_index("fsdp") * 2 + lax.axis_index("ctx") + step, 8)
    return {"fsdp": rank // 2, "ctx": lax.rem(rank, 2)}


def z_peer(step, count):
    return {"tp": lax.rem(lax.axis_index("tp") + step, count)}


def greet(peers):
    barrier = pltpu.get_barrier_semaphore()
    for peer in peers:
        pl.semaphore_signal(barrier, inc=1, device_id=peer, device_id_type=MESH)
    pl.semaphore_wait(barrier, len(peers))


def remote(src, dst, sems, k, peer):
    return pltpu.make_async_remote_copy(
        src_ref=src,
        dst_ref=dst,
        send_sem=sems[0].at[k],
        recv_sem=sems[1].at[k],
        device_id=peer,
        device_id_type=MESH,
    )


def run_all(*parts):
    parts = list(parts)
    while parts:
        parts = [part for part in parts if next(part, "end") != "end"]


def plane_gather(src, out, sems, own_sem):
    core, y, x, _ = position()
    half = src.shape[0] // 2
    first, second = pl.ds(0, half), pl.ds(half, half)

    def slot(yy, xx):
        return (yy * 2 + core) * 2 + xx

    own, from_x, from_y, diag = slot(y, x), slot(y, 1 - x), slot(1 - y, x), slot(1 - y, 1 - x)
    to_p, to_x, to_y = partner(), x_peer(), y_peer()

    def piece(k, where, rows, peer):
        place = out.at[where, rows]
        return remote(src.at[rows] if k < 4 else place, place, sems, k, peer)

    sends = [
        piece(0, own, first, to_x),
        piece(1, own, second, to_y),
        piece(2, own, second, to_x),
        piece(3, own, first, to_y),
    ]
    whole = remote(src, out.at[own], sems, 4, to_p)
    keep = pltpu.make_async_copy(src, out.at[own], own_sem)
    for copy in sends:
        copy.start()
    whole.start()
    keep.start()
    yield
    relays = [
        (0, [(5, from_x, first, to_y), (7, from_x, first, to_p)]),
        (1, [(6, from_y, second, to_x), (8, from_y, second, to_p)]),
        (2, [(9, from_x, second, to_p)]),
        (3, [(10, from_y, first, to_p)]),
    ]
    later = []
    for k, nexts in relays:
        sends[k].wait_recv()
        for args in nexts:
            copy = piece(*args)
            copy.start()
            later.append(copy)
        if k == 1:
            yield
    by_key = {5: later[0], 6: later[2]}
    yield
    for k, args in ((5, (11, diag, first, to_p)), (6, (12, diag, second, to_p))):
        by_key[k].wait_recv()
        copy = piece(*args)
        copy.start()
        later.append(copy)
    yield
    for copy in later:
        if copy is not by_key[5] and copy is not by_key[6]:
            copy.wait_recv()
    whole.wait_recv()
    for copy in sends + later + [whole]:
        copy.wait_send()
    keep.wait()


def z_gather(src, out, ups, downs, own_sem, count):
    t = lax.axis_index("tp")
    keep = pltpu.make_async_copy(src, out.at[t], own_sem)

    def up(s):
        where = out.at[jnp.maximum(t - s, 0)]
        peer = {"tp": jnp.minimum(t + 1, count - 1)}
        return remote(src if s == 0 else where, where, ups, s, peer)

    def down(s):
        where = out.at[jnp.minimum(t + s, count - 1)]
        peer = {"tp": jnp.maximum(t - 1, 0)}
        return remote(src if s == 0 else where, where, downs, s, peer)

    for s in range(count):
        if s > 0:

            @pl.when(t - s >= 0)
            def _():
                up(s - 1).wait_recv()

            @pl.when(t + s <= count - 1)
            def _():
                down(s - 1).wait_recv()

        if s < count - 1:

            @pl.when((t - s >= 0) & (t < count - 1))
            def _():
                up(s).start()

            @pl.when((t + s <= count - 1) & (t > 0))
            def _():
                down(s).start()

            if s == 0:
                keep.start()
            yield
    for s in range(count - 1):

        @pl.when((t - s >= 0) & (t < count - 1))
        def _():
            up(s).wait_send()

        @pl.when((t + s <= count - 1) & (t > 0))
        def _():
            down(s).wait_send()

    keep.wait()


def x_gather(src, out, sems, own_sem):
    x = lax.axis_index("ctx")
    copy = remote(src, out.at[x], sems, 0, x_peer())
    keep = pltpu.make_async_copy(src, out.at[x], own_sem)
    copy.start()
    keep.start()
    yield
    yield
    yield
    copy.wait()
    keep.wait()


def x_swap(src, out, sems):
    copy = remote(src.at[1 - lax.axis_index("ctx")], out, sems, 0, x_peer())
    copy.start()
    yield
    yield
    copy.wait()


def plane_scatter(src, out, core_in, summed, side_in, mixed, last_in, sems):
    core, y, x, _ = position()
    half = out.shape[0] // 2
    rows = (pl.ds(0, half), pl.ds(half, half))
    to_p, to_x, to_y = partner(), x_peer(), y_peer()
    wide = jnp.float32
    first = []
    for q in range(4):
        there = ((q // 2) * 2 + 1 - core) * 2 + q % 2
        first.append(remote(src.at[there], core_in.at[q], sems, q, to_p))
    for copy in first:
        copy.start()
    yield
    for q in range(4):
        first[q].wait_recv()
        here = ((q // 2) * 2 + core) * 2 + q % 2
        summed[q] = (src[here].astype(wide) + core_in[q].astype(wide)).astype(summed.dtype)
    second = [
        remote(summed.at[(1 - y) * 2 + 1 - x, rows[0]], side_in.at[0], sems, 4, to_x),
        remote(summed.at[(1 - y) * 2 + 1 - x, rows[1]], side_in.at[1], sems, 5, to_y),
        remote(summed.at[y * 2 + 1 - x, rows[0]], side_in.at[2], sems, 6, to_x),
        remote(summed.at[(1 - y) * 2 + x, rows[1]], side_in.at[3], sems, 7, to_y),
    ]
    for copy in second:
        copy.start()
    yield
    third = []
    for k, (where, peer) in enumerate((((1 - y) * 2 + x, to_y), (y * 2 + 1 - x, to_x))):
        second[k].wait_recv()
        total = summed[where, rows[k]].astype(wide) + side_in[k].astype(wide)
        mixed[k] = total.astype(mixed.dtype)
        copy = remote(mixed.at[k], last_in.at[k], sems, 8 + k, peer)
        copy.start()
        third.append(copy)
    yield
    for k in range(2):
        second[2 + k].wait_recv()
        third[k].wait_recv()
        out[rows[k]] = (
            summed[y * 2 + x, rows[k]].astype(wide)
            + side_in[2 + k].astype(wide)
            + last_in[k].astype(wide)
        )
    for copy in first + second + third:
        copy.wait_send()


def z_scatter(src, out, landed, sems, count):
    t = lax.axis_index("tp")
    copies = []
    for d in range(1, count):
        peer = z_peer(d, count)
        copies.append(remote(src.at[peer["tp"]], landed.at[d - 1], sems, d - 1, peer))
    for copy in copies:
        copy.start()
    yield
    yield
    yield
    total = src[t].astype(jnp.float32)
    for d in range(1, count):
        copies[d - 1].wait()
        total = total + landed[d - 1].astype(jnp.float32)
    out[...] = total


def small_sum(src, out, z_in, middle, plane_in, z_sems, plane_sems, count, shared):
    t = lax.axis_index("tp")
    rank = lax.axis_index("fsdp") * 2 + lax.axis_index("ctx")
    ones = [remote(src, z_in.at[t], z_sems, d - 1, z_peer(d, count)) for d in range(1, count)]
    for copy in ones:
        copy.start()
    z_in[t] = src[...]
    yield
    for copy in ones:
        copy.wait()
    total = z_in[0]
    for i in range(1, count):
        total = total + z_in[i]
    row = lax.broadcasted_iota(jnp.int32, total.shape, 0)
    middle[...] = jnp.where(row < shared, total, src[...])
    twos = [remote(middle, plane_in.at[rank], plane_sems, d - 1, plane_peer(d)) for d in range(1, 8)]
    for copy in twos:
        copy.start()
    plane_in[rank] = middle[...]
    yield
    yield
    for copy in twos:
        copy.wait()
    total = plane_in[0]
    for i in range(1, 8):
        total = total + plane_in[i]
    out[...] = total


def near_peers(count):
    return [partner(), x_peer(), y_peer()] + [z_peer(d, count) for d in range(1, count)]


def sem_pair(count):
    return [pltpu.SemaphoreType.DMA((count,)), pltpu.SemaphoreType.DMA((count,))]


def call(body, outs, out_specs, inputs, scratch, collective):
    return pl.pallas_call(
        body,
        out_shape=outs,
        in_specs=[VMEM] * len(inputs),
        out_specs=out_specs,
        scratch_shapes=scratch,
        compiler_params=pltpu.CompilerParams(
            collective_id=collective, has_side_effects=True, vmem_limit_bytes=48 * 1024 * 1024
        ),
    )(*inputs)


def shape(dims, dtype=jnp.bfloat16):
    return jax.ShapeDtypeStruct(dims, dtype)


def gather_first(weights, rows, count):
    def body(w, r, wf, rf, a, b, c, d, e, g, own):
        greet(near_peers(count))
        run_all(
            z_gather(r, rf, (c, d), (e, g), own.at[0], count),
            plane_gather(w, wf, (a, b), own.at[1]),
        )

    return call(
        body,
        [shape((8,) + weights.shape), shape((count,) + rows.shape)],
        [ANY, ANY],
        (weights, rows),
        sem_pair(13) + sem_pair(count) + sem_pair(count) + [pltpu.SemaphoreType.DMA((2,))],
        0,
    )


def gather_second(rows, keys, count):
    def body(r, k, rf, kf, a, b, c, d, e, g, own):
        greet(near_peers(count))
        run_all(
            z_gather(r, rf, (c, d), (e, g), own.at[0], count),
            x_gather(k, kf, (a, b), own.at[1]),
        )

    return call(
        body,
        [shape((count,) + rows.shape), shape((2,) + keys.shape)],
        [ANY, ANY],
        (rows, keys),
        sem_pair(1) + sem_pair(count) + sem_pair(count) + [pltpu.SemaphoreType.DMA((2,))],
        1,
    )


def scatter_scratch(block):
    rows, lanes = block
    half = rows // 2
    return [
        pltpu.VMEM((4, rows, lanes), jnp.bfloat16),
        pltpu.VMEM((4, rows, lanes), jnp.bfloat16),
        pltpu.VMEM((4, half, lanes), jnp.bfloat16),
        pltpu.VMEM((2, half, lanes), jnp.bfloat16),
        pltpu.VMEM((2, half, lanes), jnp.bfloat16),
    ] + sem_pair(10)


def scatter_first(grads, partial, key_grads, count):
    def body(g, p, k, go, po, ko, a, b, c, d, e, s0, s1, land, z0, z1, x0, x1):
        greet(near_peers(count))
        run_all(
            plane_scatter(g, go, a, b, c, d, e, (s0, s1)),
            x_swap(k, ko, (x0, x1)),
            z_scatter(p, po, land, (z0, z1), count),
        )

    return call(
        body,
        [
            shape(grads.shape[1:], jnp.float32),
            shape(partial.shape[1:], jnp.float32),
            shape(key_grads.shape[1:]),
        ],
        [VMEM] * 3,
        (grads, partial, key_grads),
        scatter_scratch(grads.shape[1:])
        + [pltpu.VMEM((count - 1,) + partial.shape[1:], jnp.bfloat16)]
        + sem_pair(count)
        + sem_pair(1),
        2,
    )


def scatter_second(grads, partial, small, count, shared):
    def body(g, p, m, go, po, mo, a, b, c, d, e, s0, s1, land, z0, z1, zi, mid, pi, m0, m1, n0, n1):
        greet(
            [plane_peer(i) for i in range(1, 8)] + [z_peer(i, count) for i in range(1, count)]
        )
        run_all(
            small_sum(m, mo, zi, mid, pi, (m0, m1), (n0, n1), count, shared),
            plane_scatter(g, go, a, b, c, d, e, (s0, s1)),
            z_scatter(p, po, land, (z0, z1), count),
        )

    return call(
        body,
        [
            shape(grads.shape[1:], jnp.float32),
            shape(partial.shape[1:], jnp.float32),
            shape(small.shape, jnp.float32),
        ],
        [VMEM] * 3,
        (grads, partial, small),
        scatter_scratch(grads.shape[1:])
        + [pltpu.VMEM((count - 1,) + partial.shape[1:], jnp.bfloat16)]
        + sem_pair(count)
        + [
            pltpu.VMEM((count,) + small.shape, jnp.float32),
            pltpu.VMEM(small.shape, jnp.float32),
            pltpu.VMEM((8,) + small.shape, jnp.float32),
        ]
        + sem_pair(count)
        + sem_pair(7),
        3,
    )


def plain_gather_first(weights, rows, count):
    return lax.all_gather(weights, PLANE), lax.all_gather(rows, "tp")


def plain_gather_second(rows, keys, count):
    return lax.all_gather(rows, "tp"), lax.all_gather(keys, "ctx")


def plain_scatter(grads, partial):
    grads = lax.psum_scatter(grads.astype(jnp.float32), PLANE, scatter_dimension=0)
    return grads, lax.psum_scatter(partial.astype(jnp.float32), "tp", scatter_dimension=0)


def plain_scatter_first(grads, partial, key_grads, count):
    x = lax.axis_index("ctx")
    total = lax.psum_scatter(key_grads.astype(jnp.float32), "ctx", scatter_dimension=0)
    own = lax.dynamic_index_in_dim(key_grads, x, 0, keepdims=False)
    return plain_scatter(grads, partial) + (total - own.astype(jnp.float32),)


def plain_scatter_second(grads, partial, small, count, shared):
    total = lax.psum(small, PLANE)
    return plain_scatter(grads, partial) + (
        jnp.concatenate([lax.psum(total[:shared], "tp"), total[shared:]]),
    )


def attention_probs(queries, keys_all, query_pos, query_start):
    score_scale = HD ** (-0.5)
    scores = (
        jnp.einsum("qhd,khd->hqk", queries, keys_all, preferred_element_type=jnp.float32)
        * score_scale
    )
    key_pos = jnp.arange(keys_all.shape[0], dtype=jnp.int32)
    allowed = (key_pos[None, :] >= query_start[:, None]) & (key_pos[None, :] <= query_pos[:, None])
    masked = jnp.where(allowed[None], scores, -1e30)
    row_peak = jnp.max(masked, axis=2, keepdims=True)
    exponent = jnp.where(allowed[None], jnp.exp(masked - row_peak), 0.0)
    return exponent / jnp.sum(exponent, axis=2, keepdims=True)


def dot(a, b, dims=((1,), (0,))):
    return lax.dot_general(a, b, (dims, ((), ())), preferred_element_type=jnp.float32)


def local(
    sizes,
    block_input,
    cotangent,
    norm1_gain,
    norm1_bias,
    norm2_gain,
    norm2_bias,
    qkv_weight,
    qkv_bias,
    out_weight,
    out_bias,
    up_weight,
    up_bias,
    down_weight,
    down_bias,
    doc_ids,
    doc_start,
):
    fsdp, ctx, count = sizes
    if fsdp == 4 and ctx == 2 and count > 1:
        comm = (gather_first, gather_second, scatter_first, scatter_second)
    else:
        comm = (plain_gather_first, plain_gather_second, plain_scatter_first, plain_scatter_second)
    wide, narrow = jnp.float32, jnp.bfloat16
    own_count, width = block_input.shape
    lw = qkv_weight.shape[2]
    hidden = up_weight.shape[1]
    heads_here = lw // HD
    row_count = own_count * count
    group = fsdp * ctx
    score_scale = HD ** (-0.5)
    piece = qkv_weight.shape[1]
    packed = jnp.concatenate(
        [qkv_weight[0], qkv_weight[1], qkv_weight[2], out_weight.T, up_weight, down_weight.T],
        axis=1,
    )
    packed, full_in = comm[0](packed, block_input, count)
    packed = packed.reshape(width, packed.shape[2])
    full_in = full_in.reshape(row_count, width)
    qkv_full = packed[:, : 3 * lw]
    out_t = packed[:, 3 * lw : 4 * lw]
    up_full = packed[:, 4 * lw : 4 * lw + hidden]
    down_t = packed[:, 4 * lw + hidden :]
    gain_one = norm1_gain.astype(wide)
    gain_two = norm2_gain.astype(wide)
    normed, inv_std = normalize(full_in.astype(wide))
    first_in = (normed * gain_one + norm1_bias.astype(wide)).astype(narrow)
    second_in = (normed * gain_two + norm2_bias.astype(wide)).astype(narrow)
    projected = dot(first_in, qkv_full) + qkv_bias.astype(wide).reshape(1, 3 * lw)
    query_pos = lax.axis_index("ctx") * row_count + jnp.arange(row_count, dtype=jnp.int32)
    cosine, sine_table = angle_tables(query_pos - doc_start)
    queries = rotate(
        projected[:, :lw].reshape(row_count, heads_here, HD), cosine, sine_table
    ).astype(narrow)
    keys_here = rotate(
        projected[:, lw : 2 * lw].reshape(row_count, heads_here, HD), cosine, sine_table
    ).astype(narrow)
    keys_values = jnp.concatenate(
        [keys_here.reshape(row_count, lw), projected[:, 2 * lw :].astype(narrow)], axis=1
    )
    full_cot, keys_values = comm[1](cotangent, keys_values, count)
    full_cot = full_cot.reshape(row_count, width)
    length = ctx * row_count
    keys_values = keys_values.reshape(length, 2 * lw)
    keys_all = keys_values[:, :lw].reshape(length, heads_here, HD)
    values_all = keys_values[:, lw:].reshape(length, heads_here, HD)
    attn_probs = attention_probs(queries, keys_all, query_pos, doc_start)
    probs_b = attn_probs.astype(narrow)
    attended = jnp.einsum("hqk,khd->qhd", probs_b, values_all, preferred_element_type=wide)
    attended = attended.reshape(row_count, lw).astype(narrow)
    pre_act = dot(second_in, up_full) + up_bias.astype(wide)
    activated, gelu_slope = gelu_parts(pre_act)
    act_b = activated.astype(narrow)
    last = ((1,), (1,))
    rows = ((0,), (0,))
    forward = dot(attended, out_t, last) + dot(act_b, down_t, last)
    d_attended = dot(full_cot, out_t).astype(narrow)
    d_pre = (dot(full_cot, down_t) * gelu_slope).astype(narrow)
    grad_up_local = dot(second_in, d_pre, rows)
    grad_down_local = dot(full_cot, act_b, rows)
    up_bias_grad = jnp.sum(d_pre.astype(wide), axis=0)
    d_heads = d_attended.reshape(row_count, heads_here, HD)
    d_values = jnp.einsum("hqk,qhd->khd", probs_b, d_heads, preferred_element_type=wide)
    d_probs = jnp.einsum("qhd,khd->hqk", d_heads, values_all, preferred_element_type=wide)
    delta_sum = jnp.sum(attn_probs * d_probs, axis=2, keepdims=True)
    d_scores = (attn_probs * (d_probs - delta_sum)).astype(narrow)
    d_query = (
        jnp.einsum("hqk,khd->qhd", d_scores, keys_all, preferred_element_type=wide) * score_scale
    )
    d_keys = (
        jnp.einsum("hqk,qhd->khd", d_scores, queries, preferred_element_type=wide) * score_scale
    )
    key_grads = jnp.concatenate([d_keys.reshape(length, lw), d_values.reshape(length, lw)], axis=1)
    key_grads = key_grads.reshape(ctx, row_count, 2 * lw)
    mlp_grads, summed, key_far = comm[2](
        jnp.concatenate([grad_up_local.astype(narrow), grad_down_local.astype(narrow)], axis=1)
        .reshape(group, piece, 2 * hidden),
        forward.astype(narrow).reshape(count, own_count, width),
        key_grads.astype(narrow),
        count,
    )
    block_output = (
        block_input.astype(wide) + summed + out_bias.astype(wide) + down_bias.astype(wide)
    ).astype(narrow)
    key_own = lax.dynamic_index_in_dim(key_grads, lax.axis_index("ctx"), 0, keepdims=False)
    key_own = key_own + key_far.astype(wide)
    d_qkv = jnp.concatenate(
        [
            rotate(d_query, cosine, -sine_table).reshape(row_count, lw),
            rotate(
                key_own[:, :lw].reshape(row_count, heads_here, HD), cosine, -sine_table
            ).reshape(row_count, lw),
            key_own[:, lw:],
        ],
        axis=1,
    ).astype(narrow)
    qkv_bias_grad = jnp.sum(d_qkv.astype(wide), axis=0)
    grad_qkv_local = dot(first_in, d_qkv, rows)
    grad_out_local = dot(full_cot, attended, rows)
    d_first = dot(d_qkv, qkv_full, last)
    d_second = dot(d_pre, up_full, last)
    cot_float = cotangent.astype(wide)
    span = max(width, hidden, 3 * lw)

    def pad(row):
        return jnp.pad(row, (0, span - row.shape[0]))

    small = jnp.stack(
        [
            pad(row)
            for row in (
                jnp.sum(cot_float, axis=0),
                jnp.sum(d_first * normed, axis=0),
                jnp.sum(d_first, axis=0),
                jnp.sum(d_second * normed, axis=0),
                jnp.sum(d_second, axis=0),
                up_bias_grad,
                qkv_bias_grad,
                jnp.zeros((width,), wide),
            )
        ]
    )
    partial = d_first * gain_one + d_second * gain_two
    attn_grads, combined, small = comm[3](
        jnp.concatenate([grad_qkv_local.astype(narrow), grad_out_local.astype(narrow)], axis=1)
        .reshape(group, piece, 4 * lw),
        partial.astype(narrow).reshape(count, own_count, width),
        small,
        count,
        5,
    )
    normed_own, inv_own = normalize(block_input.astype(wide))
    mean_one = jnp.mean(combined, axis=1, keepdims=True)
    mean_two = jnp.mean(combined * normed_own, axis=1, keepdims=True)
    grad_input = (cot_float + inv_own * (combined - mean_one - normed_own * mean_two)).astype(narrow)
    return (
        block_output,
        grad_input,
        attn_grads[:, : 3 * lw].reshape(piece, 3, lw).transpose(1, 0, 2),
        small[6, : 3 * lw].reshape(3, lw),
        attn_grads[:, 3 * lw :].T,
        small[0, :width],
        mlp_grads[:, :hidden],
        small[5, :hidden],
        mlp_grads[:, hidden:].T,
        small[0, :width],
        small[1, :width],
        small[2, :width],
        small[3, :width],
        small[4, :width],
    )


def solution(mesh):
    in_specs = (
        P(("fsdp", "ctx", "tp"), None),
        P(("fsdp", "ctx", "tp"), None),
        P(),
        P(),
        P(),
        P(),
        P(None, ("fsdp", "ctx"), "tp"),
        P(None, "tp"),
        P("tp", ("fsdp", "ctx")),
        P(),
        P(("fsdp", "ctx"), "tp"),
        P("tp"),
        P("tp", ("fsdp", "ctx")),
        P(),
        P(("fsdp", "ctx")),
        P(("fsdp", "ctx")),
    )
    out_specs = (
        P(("fsdp", "ctx", "tp"), None),
        P(("fsdp", "ctx", "tp"), None),
        P(None, ("fsdp", "ctx"), "tp"),
        P(None, "tp"),
        P("tp", ("fsdp", "ctx")),
        P(),
        P(("fsdp", "ctx"), "tp"),
        P("tp"),
        P("tp", ("fsdp", "ctx")),
        P(),
        P(),
        P(),
        P(),
        P(),
    )
    sizes = tuple(mesh.shape[axis] for axis in ("fsdp", "ctx", "tp"))
    body = functools.partial(local, sizes)
    return jax.shard_map(body, mesh=mesh, in_specs=in_specs, out_specs=out_specs, check_vma=False)
```

time: 532 us -> 164 us (0.31)
  waiting for transfers between devices: 282 us -> 0 us
  blocking collectives: 154 us -> 0 us
  Pallas kernels: 0 us -> 85 us
  between operations: 16.4 us -> 1.77 us
    psum x1 -> x0, waiting for transfers between devices: 121 us -> none  [local(): first_all, second_all = lax.psum((d_first, d_second), 'tp')]
    reduce_scatter x6 -> x0, waiting for transfers between devices: 104 us -> none  [the longest x1 46.2 us: local(): lax.psum_scatter(grad_down_local, ('fsdp', 'ctx'), scatter_dimension=1, t...]
    all_gather x7 -> x0, blocking collectives: 99.9 us -> none  [the longest x1 24.7 us: local(): lax.all_gather(qkv_weight, ('fsdp', 'ctx'), axis=1, tiled=True)]
    pallas_call x0 -> x4, Pallas kernels: none -> 85 us  [call(): pl.pallas_call(body, out_shape=outs, in_specs=[VMEM] * len(inputs), out_s...]
    unnamed x13 -> x0, waiting for transfers between devices: 56.5 us -> none
    psum x2 -> x0, blocking collectives: 54.1 us -> none  [the longest x1 39.7 us: local(): lax.psum((bias_grad, jnp.sum(first_own * normed_own, axis=0), jnp.sum(fir...]
    unnamed x100 -> x106, local copies, waits for them, and re-layouts: 18.3 us -> 9.45 us
    concatenate x0 -> x7, local copies, waits for them, and re-layouts: none -> 8.89 us  [the longest x4 4.09 us: local(): jnp.concatenate([d_keys.reshape(length, lw), d_values.reshape(length, lw)...]
  transfers between devices with their start and end apart: 11 -> 0, of which waited for: 8 -> 0; matrix products, arithmetic and copies ran while one was open for 13% -> 0% of each run, Pallas kernels for 0% -> 0%
where the time goes in v1:
time: 164 us; the launch traced here: 163 us
  Pallas kernels  85 us (52%)
  matrix products  42.2 us (26%)
  local copies, waits for them, and re-layouts  24.6 us (15%)
  other arithmetic  9.34 us (6%)
  between operations  1.77 us (1%)
    pallas_call x4, Pallas kernels, call(): pl.pallas_call(body, out_shape=outs, in_specs=[VMEM] * len(inputs), out_s...  85 us
    dot_general x12, matrix products, dot(): lax.dot_general(a, b, (dims, ((), ())), preferred_element_type=jnp.float32)  20.5 us
    unnamed x106, local copies, waits for them, and re-layouts  9.45 us
    sub x1, matrix products, attention_probs(): exponent = jnp.where(allowed[None], jnp.exp(masked - row_peak), 0.0)  6.88 us
    concatenate x4, local copies, waits for them, and re-layouts, local(): jnp.concatenate([d_keys.reshape(length, lw), d_values.reshape(length, lw)...  4.09 us
    dot_general x1, matrix products, local(): jnp.einsum('hqk,khd->qhd', probs_b, values_all, preferred_element_type=wide)  3.92 us
    dot_general x1, matrix products, local(): jnp.einsum('qhd,khd->hqk', d_heads, values_all, preferred_element_type=wide)  3.73 us
    dot_general x1, matrix products, local(): jnp.einsum('hqk,qhd->khd', probs_b, d_heads, preferred_element_type=wide)  3.52 us

profile of v1, /device:TPU:0, one launch (start us, length us, event | category | flops | bytes accessed | tf_op | source)
XLA Modules:
  0.0 163.0 jit_solution(15319652631871204943)
XLA Ops:
  4.5 23.3 %shard_map.254 = (bf16[8,96,2304]{2,1,0:T(8,128)(2,1)S(1)}, bf16[4,128,768]{2,1,0:T(8,128)(2,1)S(1)}) custom-call(bf16[96,2304]{1,0:T(8,128)(2,1)S(1)} %concatenate.66.w, bf16[128,768]{1,0:T(8,128)(2,1)S(1)} %copy-done), custom_call_target="tpu_custom_call" | custom-call | tf_op jit(solution)/shard_map/pallas_call | solution.py:336
  28.5 1.4 add_convert_fusion.3
  30.0 2.2 %convolution_add_fusion.1 = f32[512,576]{1,0:T(8,128)S(1)} fusion(bf16[512,768]{1,0:T(8,128)(2,1)S(1)} %get-tuple-element.80, bf16[768,2304]{1,0:T(8,128)(2,1)} %bitcast.96, f32[576]{0:T(1024)S(1)} %reshape.284), kind=kOutput, calls=%fused_computation.46 | convolution fusion | flops 453279744 | bytes 2951424 | tf_op jit(solution)/shard_map/dot_general | solution.py:502
  34.2 19.0 %shard_map.255 = (bf16[4,128,768]{2,1,0:T(8,128)(2,1)S(1)}, bf16[2,512,384]{2,1,0:T(8,128)(2,1)S(1)}) custom-call(bf16[128,768]{1,0:T(8,128)(2,1)S(1)} %copy-done.2, bf16[512,384]{1,0:T(8,128)(2,1)S(1)} %pad_maximum_fusion.4.k), custom_call_target="tpu_custom_call" | custom-call | tf_op jit(solution)/shard_map/pallas_call | solution.py:336
  54.5 1.4 fusion.7
  56.1 6.9 %fusion.79 = (f32[3,512]{1,0:T(4,128)S(1)}, f32[3,512,1024]{2,1,0:T(8,128)}) fusion(pred[512,1024]{1,0:T(8,128)(4,1)} %fusion.7, bf16[1024,3,64]{0,2,1:T(8,128)(2,1)S(1)} %bitcast.106, bf16[512,3,48]{0,2,1:T(8,128)(2,1)S(1)} %slice.260, bf16[512,3,16]{0,2,1:T(8,128)(2,1)S(1)} %get-tuple-element.100), kind=kOutput, calls=%fused_computation.159 | convolution fusion | flops 209585152 | bytes 7411712 | tf_op jit(solution)/shard_map/sub | solution.py:497
  63.0 3.9 %fusion.25 = bf16[3,64,512]{2,1,0:T(8,128)(2,1)S(1)} fusion(bf16[1024,3,64]{0,2,1:T(8,128)(2,1)S(1)} %bitcast.123, f32[3,512,1024]{2,1,0:T(8,128)} %get-tuple-element.110, f32[3,512]{1,0:T(4,128)S(1)} %get-tuple-element.109), kind=kOutput, calls=%fused_computation.55 | convolution fusion | flops 204570624 | bytes 6887424 | tf_op jit(solution)/shard_map/hqk,khd->qhd/dot_general | solution.py:574
  68.0 1.6 convolution_convert_fusion.4
  69.6 3.7 %multiply_reduce_fusion = (f32[3,512]{1,0:T(4,128)S(1)}, f32[3,512,1024]{2,1,0:T(8,128)S(1)}) fusion(f32[3,512,1024]{2,1,0:T(8,128)} %get-tuple-element.110, f32[3,512]{1,0:T(4,128)S(1)} %get-tuple-element.109, bf16[512,3,64]{0,2,1:T(8,128)(2,1)S(1)} %bitcast.126, bf16[1024,3,64]{0,2,1:T(8,128)(2,1)S(1)} %bitcast.124), kind=kOutput, calls=%fused_computation.2 | convolution fusion | flops 206043648 | bytes 13185024 | tf_op jit(solution)/shard_map/qhd,khd->hqk/dot_general | solution.py:589
  75.5 1.7 %copy-done.8 = bf16[3,512,1024]{2,1,0:T(8,128)(2,1)} copy-done((bf16[3,512,1024]{2,1,0:T(8,128)(2,1)}, bf16[3,512,1024]{2,1,0:T(8,128)(2,1)S(1)}, u32[]{:S(2)}) %copy-start.8) | copy-done | bytes 3145752
  78.5 1.4 copy.60
  79.9 3.5 %fusion.20 = f32[1024,3,64]{0,2,1:T(8,128)S(1)} fusion(bf16[512,3,64]{0,2,1:T(8,128)(2,1)S(1)} %bitcast.127, f32[3,512,1024]{2,1,0:T(8,128)} %get-tuple-element.110, f32[3,512]{1,0:T(4,128)S(1)} %get-tuple-element.109), kind=kOutput, calls=%fused_computation.48 | convolution fusion | flops 204472320 | bytes 7280640 | tf_op jit(solution)/shard_map/hqk,qhd->khd/dot_general | solution.py:588
  84.1 1.4 copy.61
  85.5 2.1 %multiply_convert_fusion.1 = (bf16[512,768]{1,0:T(8,128)(2,1)S(1)}, f32[512,768]{1,0:T(8,128)S(1)}) fusion(f32[768]{0:T(1024)S(1)} %convert_element_type.132, bf16[512,768]{1,0:T(8,128)(2,1)S(1)} %copy-done.22, bf16[768,2304]{1,0:T(8,128)(2,1)} %bitcast.98), kind=kOutput, calls=%fused_computation.37 | convolution fusion | flops 606339072 | bytes 4328448 | tf_op jit(solution)/shard_map/dot_general | solution.py:502
  88.5 2.3 %convert_reduce_fusion = (f32[768]{0:T(1024)S(1)}, bf16[512,768]{1,0:T(8,128)(2,1)S(1)}) fusion(f32[512,768]{1,0:T(8,128)S(1)} %get-tuple-element.108, bf16[512,768]{1,0:T(8,128)(2,1)S(1)} %bitcast.92, bf16[768,2304]{1,0:T(8,128)(2,1)} %bitcast.99), kind=kOutput, calls=%fused_computation.28 | convolution fusion | flops 608697600 | bytes 4328448 | tf_op jit(solution)/shard_map/dot_general | solution.py:502
  91.8 1.6 pad_maximum_fusion
  93.4 2.8 %copy.56 = bf16[768,1536]{1,0:T(8,128)(2,1)S(1)} copy(bf16[768,1536]{0,1:T(8,128)(2,1)} %pad_maximum_fusion) | data formatting | bytes 4718592 | tf_op jit(solution)/shard_map/concatenate | solution.py:601
  96.2 1.7 %fusion.52 = f32[512,768]{1,0:T(8,128)S(1)} fusion(bf16[512,192]{0,1:T(8,128)(2,1)S(1)} %bitcast.119, bf16[768,2304]{1,0:T(8,128)(2,1)} %bitcast.100), kind=kOutput, calls=%fused_computation.91 | convolution fusion | flops 150994944 | bytes 2162688 | tf_op jit(solution)/shard_map/dot_general | solution.py:502
  97.9 2.2 %add_convert_fusion.1 = bf16[512,768]{1,0:T(8,128)(2,1)S(1)} fusion(f32[512,768]{1,0:T(8,128)S(1)} %fusion.52, bf16[512,768]{1,0:T(8,128)(2,1)S(1)} %copy-done.46, bf16[768,2304]{1,0:T(8,128)(2,1)} %bitcast.101), kind=kOutput, calls=%fused_computation.32 | convolution fusion | flops 604766208 | bytes 4325376 | tf_op jit(solution)/shard_map/dot_general | solution.py:502
  100.4 21.3 %shard_map.256 = (f32[96,1536]{1,0:T(8,128)S(1)}, f32[128,768]{1,0:T(8,128)S(1)}, bf16[512,384]{1,0:T(8,128)(2,1)S(1)}) custom-call(bf16[8,96,1536]{2,1,0:T(8,128)(2,1)S(1)} %bitcast.87, bf16[4,128,768]{2,1,0:T(8,128)(2,1)S(1)} %bitcast.95, bf16[2,512,384]{2,1,0:T(8,128)(2,1)S(1)} %fusion.8.k), custom_call_target="tpu_custom_call" | custom-call | tf_op jit(solution)/shard_map/pallas_call | solution.py:336
  123.7 3.0 %fusion.24 = f32[512,3,64]{0,2,1:T(8,128)S(1)} fusion(bf16[1024,3,64]{0,2,1:T(8,128)(2,1)S(1)} %bitcast.107, bf16[3,512,1024]{2,1,0:T(8,128)(2,1)} %copy-done.8), kind=kOutput, calls=%fused_computation.53 | convolution fusion | flops 201424896 | bytes 3932160 | tf_op jit(solution)/shard_map/hqk,khd->qhd/dot_general | solution.py:593
  129.9 2.3 %fusion.33 = f32[512,768]{1,0:T(8,128)S(1)} fusion(bf16[768,2304]{1,0:T(8,128)(2,1)} %bitcast.102, bf16[512,192]{1,0:T(8,128)(2,1)} %copy-done.18, bf16[512,192]{1,0:T(8,128)(2,1)} %copy-done.14, bf16[512,192]{1,0:T(8,128)(2,1)} %copy-done.16), kind=kOutput, calls=%fused_computation.63 | convolution fusion | flops 454754304 | bytes 3342336 | tf_op jit(solution)/shard_map/dot_general | solution.py:502
  132.3 2.5 %fusion.74 = (f32[768]{0:T(1024)S(1)}, f32[768]{0:T(1024)S(1)}, bf16[512,768]{1,0:T(8,128)(2,1)S(1)}, f32[768]{0:T(1024)S(1)}, f32[768]{0:T(1024)S(1)}) fusion(f32[512]{0:T(512)S(1)} %copy-done.36, f32[512]{0:T(512)S(1)} %copy-done.33, bf16[4,128,768]{2,1,0:T(8,128)(2,1)S(1)} %get-tuple-element.24, f32[768]{0:T(1024)S(1)} %convert_element_type.124, ...), kind=kOutput, calls=%fused_computation.154 | convolution fusion | flops 609088512 | bytes 5134336 | tf_op jit(solution)/shard_map/dot_general | solution.py:502
  135.3 21.5 %shard_map.257 = (f32[96,768]{1,0:T(8,128)S(1)}, f32[128,768]{1,0:T(8,128)S(1)}, f32[8,768]{1,0:T(8,128)S(1)}) custom-call(bf16[8,96,768]{2,1,0:T(8,128)(2,1)S(1)} %bitcast.88, bf16[4,128,768]{2,1,0:T(8,128)(2,1)S(1)} %bitcast.94, f32[8,768]{1,0:T(8,128)S(1)} %stack.35.m), custom_call_target="tpu_custom_call" | custom-call | tf_op jit(solution)/shard_map/pallas_call | solution.py:336
  (189 shorter events, 26.5 us)
Async XLA Ops:
  0.6 27.1 %copy-start.37 = (bf16[768]{0:T(1024)(128)(2,1)S(1)}, bf16[768]{0:T(1024)(128)(2,1)}, u32[]{:S(2)}) copy-start(bf16[768]{0:T(1024)(128)(2,1)} %param.21) | copy-start | bytes 4612
  0.7 27.1 %copy-start.38 = (bf16[768]{0:T(1024)(128)(2,1)S(1)}, bf16[768]{0:T(1024)(128)(2,1)}, u32[]{:S(2)}) copy-start(bf16[768]{0:T(1024)(128)(2,1)} %param.20) | copy-start | bytes 4612
  2.4 26.0 %copy-start.39 = (bf16[768]{0:T(1024)(128)(2,1)S(1)}, bf16[768]{0:T(1024)(128)(2,1)}, u32[]{:S(2)}) copy-start(bf16[768]{0:T(1024)(128)(2,1)} %param.19) | copy-start | bytes 4612
  2.4 26.0 %copy-start.40 = (bf16[768]{0:T(1024)(128)(2,1)S(1)}, bf16[768]{0:T(1024)(128)(2,1)}, u32[]{:S(2)}) copy-start(bf16[768]{0:T(1024)(128)(2,1)} %param.18) | copy-start | bytes 4612
  28.4 3.7 %copy-start.35 = (f32[512]{0:T(512)}, f32[512]{0:T(512)S(1)}, u32[]{:S(2)}) copy-start(f32[512]{0:T(512)S(1)} %rsqrt_bitcast_fusion) | copy-start | bytes 6148
  33.9 19.4 %copy-start.26 = (f32[512,16]{0,1:T(8,128)}, f32[512,16]{0,1:T(8,128)S(1)}, u32[]{:S(2)}) copy-start(f32[512,16]{0,1:T(8,128)S(1)} %get-tuple-element.104) | copy-start | bytes 98308
  56.1 6.9 %copy-start.11 = (bf16[1024,192]{0,1:T(8,128)(2,1)}, bf16[1024,192]{0,1:T(8,128)(2,1)S(1)}, u32[]{:S(2)}) copy-start(bf16[1024,192]{0,1:T(8,128)(2,1)S(1)} %copy.59) | copy-start | bytes 1179652
  56.1 6.9 %copy-start.23 = (bf16[512,3,48]{0,2,1:T(8,128)(2,1)}, bf16[512,3,48]{0,2,1:T(8,128)(2,1)S(1)}, u32[]{:S(2)}) copy-start(bf16[512,3,48]{0,2,1:T(8,128)(2,1)S(1)} %slice.260) | copy-start | bytes 442372
  56.1 6.9 %copy-start.25 = (bf16[1024,192]{0,1:T(8,128)(2,1)S(1)}, bf16[1024,192]{0,1:T(8,128)(2,1)}, u32[]{:S(2)}) copy-start(bf16[1024,192]{0,1:T(8,128)(2,1)} %copy.57) | copy-start | bytes 1179652
  69.6 3.8 %copy-start.28 = (bf16[512,192]{0,1:T(8,128)(2,1)}, bf16[512,192]{0,1:T(8,128)(2,1)S(1)}, u32[]{:S(2)}) copy-start(bf16[512,192]{0,1:T(8,128)(2,1)S(1)} %convolution_convert_fusion.4) | copy-start | bytes 589828
  69.6 4.1 %slice-start = ((s8[6291456]{0:T(1024)(128)(4,1)}), s8[4194304]{0:T(1024)(128)(4,1)S(1)}, s32[]{:S(2)}) async-start(s8[6291456]{0:T(1024)(128)(4,1)} %bitcast.104), calls=%async_computation | async-start | bytes 8388608
  69.6 4.8 %slice-start.1 = ((s8[6291456]{0:T(1024)(128)(4,1)}), s8[2097152]{0:T(1024)(128)(4,1)S(1)}, s32[]{:S(2)}) async-start(s8[6291456]{0:T(1024)(128)(4,1)} %bitcast.104), calls=%async_computation.1 | async-start | bytes 4194304
  74.4 2.7 %copy-start.24 = (bf16[512,3,48]{0,2,1:T(8,128)(2,1)S(1)}, bf16[512,3,48]{0,2,1:T(8,128)(2,1)}, u32[]{:S(2)}) copy-start(bf16[512,3,48]{0,2,1:T(8,128)(2,1)} %copy-done.23) | copy-start | bytes 442372
  122.8 4.3 %copy-start.18 = (bf16[512,192]{1,0:T(8,128)(2,1)}, bf16[512,192]{1,0:T(8,128)(2,1)S(1)}, u32[]{:S(2)}) copy-start(bf16[512,192]{1,0:T(8,128)(2,1)S(1)} %slice.256) | copy-start | bytes 589828
  123.7 3.0 %copy-start.27 = (f32[512,16]{0,1:T(8,128)S(1)}, f32[512,16]{0,1:T(8,128)}, u32[]{:S(2)}) copy-start(f32[512,16]{0,1:T(8,128)} %copy-done.26) | copy-start | bytes 98308
  123.7 3.0 %copy-start.30 = (f32[512,16]{0,1:T(8,128)S(1)}, f32[512,16]{0,1:T(8,128)}, u32[]{:S(2)}) copy-start(f32[512,16]{0,1:T(8,128)} %get-tuple-element.102) | copy-start | bytes 98308
  132.2 2.6 %copy-start.15 = (bf16[512,192]{1,0:T(8,128)(2,1)S(1)}, bf16[512,192]{1,0:T(8,128)(2,1)}, u32[]{:S(2)}) copy-start(bf16[512,192]{1,0:T(8,128)(2,1)} %copy-done.14) | copy-start | bytes 589828
  132.2 2.6 %copy-start.17 = (bf16[512,192]{1,0:T(8,128)(2,1)S(1)}, bf16[512,192]{1,0:T(8,128)(2,1)}, u32[]{:S(2)}) copy-start(bf16[512,192]{1,0:T(8,128)(2,1)} %copy-done.16) | copy-start | bytes 589828
  132.3 2.6 %copy-start.19 = (bf16[512,192]{1,0:T(8,128)(2,1)S(1)}, bf16[512,192]{1,0:T(8,128)(2,1)}, u32[]{:S(2)}) copy-start(bf16[512,192]{1,0:T(8,128)(2,1)} %copy-done.18) | copy-start | bytes 589828
  134.7 22.0 %copy-start.1 = (bf16[128,768]{1,0:T(8,128)(2,1)S(1)}, bf16[128,768]{1,0:T(8,128)(2,1)}, u32[]{:S(2)}) copy-start(bf16[128,768]{1,0:T(8,128)(2,1)} %r.2) | copy-start | bytes 589828
  135.2 22.2 %copy-start.43 = (bf16[768]{0:T(1024)(128)(2,1)S(1)}, bf16[768]{0:T(1024)(128)(2,1)}, u32[]{:S(2)}) copy-start(bf16[768]{0:T(1024)(128)(2,1)} %param.29) | copy-start | bytes 4612
  135.2 22.2 %copy-start.44 = (bf16[768]{0:T(1024)(128)(2,1)S(1)}, bf16[768]{0:T(1024)(128)(2,1)}, u32[]{:S(2)}) copy-start(bf16[768]{0:T(1024)(128)(2,1)} %param.25) | copy-start | bytes 4612
  135.2 22.2 %copy-start.6 = (f32[128,768]{1,0:T(8,128)S(1)}, f32[128,768]{1,0:T(8,128)}, u32[]{:S(2)}) copy-start(f32[128,768]{1,0:T(8,128)} %copy-done.5) | copy-start | bytes 1179652
  157.4 4.1 %copy-start.4 = (f32[96,1536]{1,0:T(8,128)S(1)}, f32[96,1536]{1,0:T(8,128)}, u32[]{:S(2)}) copy-start(f32[96,1536]{1,0:T(8,128)} %copy-done.3) | copy-start | bytes 1769476
  (27 other events, 41.8 us)

commit v2 on v1

--- a/solution.py
+++ b/solution.py
@@ -173,6 +173,8 @@
         return remote(src if s == 0 else where, where, downs, s, peer)
 
     for s in range(count):
+        if s == count - 1:
+            yield
         if s > 0:
 
             @pl.when(t - s >= 0)
@@ -209,8 +211,33 @@
     keep.wait()
 
 
-def x_gather(src, out, sems, own_sem):
+def head_lanes(h, base=0):
+    return slice(base + h * HD, base + (h + 1) * HD)
+
+
+def row_tiles(rows):
+    return 2 if rows % 32 == 0 else 1
+
+
+def attend(queries, keys, values, starts, out, first_row, wait):
+    wait()
+    rows, lw = queries.shape
+    tile = rows // row_tiles(rows)
+    for h in range(lw // HD):
+        for r in range(0, rows, tile):
+            here = pl.ds(r, tile)
+            probs = head_probs(
+                queries[here, head_lanes(h)], keys(h), starts[here, :], first_row + r
+            )
+            out[here, head_lanes(h)] = dot(probs.astype(jnp.bfloat16), values(h)).astype(
+                jnp.bfloat16
+            )
+    yield
+
+
+def x_gather_attend(src, out, sems, own_sem, queries, starts, attended):
     x = lax.axis_index("ctx")
+    rows, lanes = src.shape
     copy = remote(src, out.at[x], sems, 0, x_peer())
     keep = pltpu.make_async_copy(src, out.at[x], own_sem)
     copy.start()
@@ -218,16 +245,55 @@
     yield
     yield
     yield
+    yield
+
+    def wait():
+        copy.wait()
+        keep.wait()
+
+    def keys(h):
+        return out[:, :, head_lanes(h)].reshape(2 * rows, HD)
+
+    def values(h):
+        return out[:, :, head_lanes(h, lanes // 2)].reshape(2 * rows, HD)
+
+    yield from attend(queries, keys, values, starts, attended, x * rows, wait)
+
+
+def attend_back(queries, kv, d_out, starts, d_query, key_sum, total, far, landed, sems):
+    x = lax.axis_index("ctx")
+    rows, lw = queries.shape
+    tile = rows // row_tiles(rows)
+    yield
+    for h in range(lw // HD):
+        keys = kv[:, head_lanes(h)]
+        values = kv[:, head_lanes(h, lw)]
+        for r in range(0, rows, tile):
+            here = pl.ds(r, tile)
+            dq, dk, dv = head_back(
+                queries[here, head_lanes(h)],
+                keys,
+                values,
+                d_out[here, head_lanes(h)],
+                starts[here, :],
+                x * rows + r,
+            )
+            d_query[here, head_lanes(h)] = dq
+            if r == 0:
+                total[:, head_lanes(h)] = dk
+                total[:, head_lanes(h, lw)] = dv
+            else:
+                total[:, head_lanes(h)] += dk
+                total[:, head_lanes(h, lw)] += dv
+            yield
+    away = pl.ds(pl.multiple_of((1 - x) * rows, rows), rows)
+    near = pl.ds(pl.multiple_of(x * rows, rows), rows)
+    far[...] = total[away, :].astype(far.dtype)
+    copy = remote(far, landed, sems, 0, x_peer())
+    copy.start()
+    yield
     copy.wait()
-    keep.wait()
-
-
-def x_swap(src, out, sems):
-    copy = remote(src.at[1 - lax.axis_index("ctx")], out, sems, 0, x_peer())
-    copy.start()
-    yield
-    yield
-    copy.wait()
+    key_sum[...] = total[near, :] + landed[...].astype(jnp.float32)
 
 
 def plane_scatter(src, out, core_in, summed, side_in, mixed, last_in, sems):
@@ -277,22 +343,72 @@
         copy.wait_send()
 
 
-def z_scatter(src, out, landed, sems, count):
+def z_scatter(src, out, up_in, down_in, up_mix, down_mix, ups, downs, count):
     t = lax.axis_index("tp")
-    copies = []
-    for d in range(1, count):
-        peer = z_peer(d, count)
-        copies.append(remote(src.at[peer["tp"]], landed.at[d - 1], sems, d - 1, peer))
-    for copy in copies:
-        copy.start()
-    yield
-    yield
-    yield
-    total = src[t].astype(jnp.float32)
-    for d in range(1, count):
-        copies[d - 1].wait()
-        total = total + landed[d - 1].astype(jnp.float32)
-    out[...] = total
+    above = {"tp": jnp.minimum(t + 1, count - 1)}
+    below = {"tp": jnp.maximum(t - 1, 0)}
+    wide = jnp.float32
+
+    def up(b, from_ref):
+        return remote(from_ref.at[b], up_in.at[b], ups, b, above)
+
+    def down(b, from_ref):
+        return remote(from_ref.at[b], down_in.at[b], downs, b, below)
+
+    @pl.when(t == 0)
+    def _():
+        for b in range(count - 1, 0, -1):
+            up(b, src).start()
+
+    @pl.when(t == count - 1)
+    def _():
+        for b in range(count - 1):
+            down(b, src).start()
+
+    yield
+    for i in range(count - 2):
+        b = count - 1 - i
+
+        @pl.when((t < b) & (t > 0))
+        def _():
+            up(b, up_mix).wait_recv()
+            up_mix[b] = (src[b].astype(wide) + up_in[b].astype(wide)).astype(up_mix.dtype)
+            up(b, up_mix).start()
+
+        @pl.when((t > i) & (t < count - 1))
+        def _():
+            down(i, down_mix).wait_recv()
+            down_mix[i] = (src[i].astype(wide) + down_in[i].astype(wide)).astype(down_mix.dtype)
+            down(i, down_mix).start()
+
+        yield
+    out[...] = src[t].astype(wide)
+    for b in range(count):
+        if b > 0:
+
+            @pl.when(t == b)
+            def _():
+                up(b, up_mix).wait_recv()
+                out[...] += up_in[b].astype(wide)
+
+            @pl.when(t < b)
+            def _():
+                up(b, up_mix).wait_send()
+
+        if b < count - 1:
+
+            @pl.when(t == b)
+            def _():
+                down(b, down_mix).wait_recv()
+                out[...] += down_in[b].astype(wide)
+
+            @pl.when(t > b)
+            def _():
+                down(b, down_mix).wait_send()
+
+
+def z_scratch(block, count):
+    return [pltpu.VMEM((count,) + block, jnp.bfloat16)] * 4 + sem_pair(count) + sem_pair(count)
 
 
 def small_sum(src, out, z_in, middle, plane_in, z_sems, plane_sems, count, shared):
@@ -367,20 +483,30 @@
     )
 
 
-def gather_second(rows, keys, count):
-    def body(r, k, rf, kf, a, b, c, d, e, g, own):
+def gather_second(weights, rows, keys, queries, starts, count):
+    def body(w, r, k, q, st, wf, rf, kf, at, w0, w1, a, b, c, d, e, g, own):
         greet(near_peers(count))
         run_all(
+            x_gather_attend(k, kf, (a, b), own.at[1], q, st, at),
+            plane_gather(w, wf, (w0, w1), own.at[2]),
             z_gather(r, rf, (c, d), (e, g), own.at[0], count),
-            x_gather(k, kf, (a, b), own.at[1]),
         )
 
     return call(
         body,
-        [shape((count,) + rows.shape), shape((2,) + keys.shape)],
-        [ANY, ANY],
-        (rows, keys),
-        sem_pair(1) + sem_pair(count) + sem_pair(count) + [pltpu.SemaphoreType.DMA((2,))],
+        [
+            shape((8,) + weights.shape),
+            shape((count,) + rows.shape),
+            shape((2,) + keys.shape),
+            shape(queries.shape),
+        ],
+        [ANY, ANY, VMEM, VMEM],
+        (weights, rows, keys, queries, starts),
+        sem_pair(13)
+        + sem_pair(1)
+        + sem_pair(count)
+        + sem_pair(count)
+        + [pltpu.SemaphoreType.DMA((3,))],
         1,
     )
 
@@ -397,41 +523,53 @@
     ] + sem_pair(10)
 
 
-def scatter_first(grads, partial, key_grads, count):
-    def body(g, p, k, go, po, ko, a, b, c, d, e, s0, s1, land, z0, z1, x0, x1):
+def scatter_first(grads, partial, queries, kv, d_out, starts, count):
+    def body(
+        g, p, q, k, do, st, go, po, dq, ks,
+        a, b, c, d, e, s0, s1, z0, z1, z2, z3, u0, u1, v0, v1, total, far, land, x0, x1,
+    ):
         greet(near_peers(count))
         run_all(
+            z_scatter(p, po, z0, z1, z2, z3, (u0, u1), (v0, v1), count),
             plane_scatter(g, go, a, b, c, d, e, (s0, s1)),
-            x_swap(k, ko, (x0, x1)),
-            z_scatter(p, po, land, (z0, z1), count),
+            attend_back(q, k, do, st, dq, ks, total, far, land, (x0, x1)),
         )
 
+    rows, lw = queries.shape
     return call(
         body,
         [
             shape(grads.shape[1:], jnp.float32),
             shape(partial.shape[1:], jnp.float32),
-            shape(key_grads.shape[1:]),
+            shape(queries.shape, jnp.float32),
+            shape((rows, 2 * lw), jnp.float32),
         ],
-        [VMEM] * 3,
-        (grads, partial, key_grads),
+        [VMEM] * 4,
+        (grads, partial, queries, kv, d_out, starts),
         scatter_scratch(grads.shape[1:])
-        + [pltpu.VMEM((count - 1,) + partial.shape[1:], jnp.bfloat16)]
-        + sem_pair(count)
+        + z_scratch(partial.shape[1:], count)
+        + [
+            pltpu.VMEM(kv.shape, jnp.float32),
+            pltpu.VMEM((rows, 2 * lw), jnp.bfloat16),
+            pltpu.VMEM((rows, 2 * lw), jnp.bfloat16),
+        ]
         + sem_pair(1),
         2,
     )
 
 
 def scatter_second(grads, partial, small, count, shared):
-    def body(g, p, m, go, po, mo, a, b, c, d, e, s0, s1, land, z0, z1, zi, mid, pi, m0, m1, n0, n1):
+    def body(
+        g, p, m, go, po, mo,
+        a, b, c, d, e, s0, s1, z0, z1, z2, z3, u0, u1, v0, v1, zi, mid, pi, m0, m1, n0, n1,
+    ):
         greet(
             [plane_peer(i) for i in range(1, 8)] + [z_peer(i, count) for i in range(1, count)]
         )
         run_all(
             small_sum(m, mo, zi, mid, pi, (m0, m1), (n0, n1), count, shared),
             plane_scatter(g, go, a, b, c, d, e, (s0, s1)),
-            z_scatter(p, po, land, (z0, z1), count),
+            z_scatter(p, po, z0, z1, z2, z3, (u0, u1), (v0, v1), count),
         )
 
     return call(
@@ -444,8 +582,7 @@
         [VMEM] * 3,
         (grads, partial, small),
         scatter_scratch(grads.shape[1:])
-        + [pltpu.VMEM((count - 1,) + partial.shape[1:], jnp.bfloat16)]
-        + sem_pair(count)
+        + z_scratch(partial.shape[1:], count)
         + [
             pltpu.VMEM((count,) + small.shape, jnp.float32),
             pltpu.VMEM(small.shape, jnp.float32),
@@ -461,8 +598,17 @@
     return lax.all_gather(weights, PLANE), lax.all_gather(rows, "tp")
 
 
-def plain_gather_second(rows, keys, count):
-    return lax.all_gather(rows, "tp"), lax.all_gather(keys, "ctx")
+def plain_gather_second(weights, rows, keys, queries, starts, count):
+    kv = lax.all_gather(keys, "ctx")
+    whole = kv.reshape(-1, keys.shape[1])
+    lw = queries.shape[1]
+    first_row = lax.axis_index("ctx") * queries.shape[0]
+    heads = []
+    for h in range(lw // HD):
+        probs = head_probs(queries[:, head_lanes(h)], whole[:, head_lanes(h)], starts, first_row)
+        heads.append(dot(probs.astype(jnp.bfloat16), whole[:, head_lanes(h, lw)]))
+    attended = jnp.concatenate(heads, axis=1).astype(jnp.bfloat16)
+    return lax.all_gather(weights, PLANE), lax.all_gather(rows, "tp"), kv, attended
 
 
 def plain_scatter(grads, partial):
@@ -470,11 +616,24 @@
     return grads, lax.psum_scatter(partial.astype(jnp.float32), "tp", scatter_dimension=0)
 
 
-def plain_scatter_first(grads, partial, key_grads, count):
-    x = lax.axis_index("ctx")
-    total = lax.psum_scatter(key_grads.astype(jnp.float32), "ctx", scatter_dimension=0)
-    own = lax.dynamic_index_in_dim(key_grads, x, 0, keepdims=False)
-    return plain_scatter(grads, partial) + (total - own.astype(jnp.float32),)
+def plain_scatter_first(grads, partial, queries, kv, d_out, starts, count):
+    rows, lw = queries.shape
+    first_row = lax.axis_index("ctx") * rows
+    heads = [
+        head_back(
+            queries[:, head_lanes(h)],
+            kv[:, head_lanes(h)],
+            kv[:, head_lanes(h, lw)],
+            d_out[:, head_lanes(h)],
+            starts,
+            first_row,
+        )
+        for h in range(lw // HD)
+    ]
+    d_query = jnp.concatenate([head[0] for head in heads], axis=1)
+    total = jnp.concatenate([head[1] for head in heads] + [head[2] for head in heads], axis=1)
+    total = lax.psum_scatter(total, "ctx", scatter_dimension=0, tiled=True)
+    return plain_scatter(grads, partial) + (d_query, total)
 
 
 def plain_scatter_second(grads, partial, small, count, shared):
@@ -484,18 +643,27 @@
     )
 
 
-def attention_probs(queries, keys_all, query_pos, query_start):
-    score_scale = HD ** (-0.5)
-    scores = (
-        jnp.einsum("qhd,khd->hqk", queries, keys_all, preferred_element_type=jnp.float32)
-        * score_scale
-    )
-    key_pos = jnp.arange(keys_all.shape[0], dtype=jnp.int32)
-    allowed = (key_pos[None, :] >= query_start[:, None]) & (key_pos[None, :] <= query_pos[:, None])
-    masked = jnp.where(allowed[None], scores, -1e30)
-    row_peak = jnp.max(masked, axis=2, keepdims=True)
-    exponent = jnp.where(allowed[None], jnp.exp(masked - row_peak), 0.0)
-    return exponent / jnp.sum(exponent, axis=2, keepdims=True)
+def head_probs(queries, keys, starts, first_row):
+    scores = dot(queries, keys, ((1,), (1,))) * HD ** (-0.5)
+    query_pos = first_row + lax.broadcasted_iota(jnp.int32, scores.shape, 0)
+    key_pos = lax.broadcasted_iota(jnp.int32, scores.shape, 1)
+    masked = jnp.where((key_pos >= starts) & (key_pos <= query_pos), scores, -1e30)
+    exponent = jnp.exp(masked - jnp.max(masked, axis=1, keepdims=True))
+    return exponent * (1.0 / jnp.sum(exponent, axis=1, keepdims=True))
+
+
+def head_back(queries, keys, values, d_out, starts, first_row):
+    probs = head_probs(queries, keys, starts, first_row)
+    d_probs = dot(d_out, values, ((1,), (1,)))
+    delta = jnp.sum(probs * d_probs, axis=1, keepdims=True)
+    d_scores = (probs * (d_probs - delta)).astype(jnp.bfloat16)
+    scale = HD ** (-0.5)
+    d_values = dot(probs.astype(jnp.bfloat16), d_out, ((0,), (0,)))
+    return (
+        dot(d_scores, keys) * scale,
+        dot(d_scores, queries, ((0,), (0,))) * scale,
+        d_values,
+    )
 
 
 def dot(a, b, dims=((1,), (0,))):
@@ -533,19 +701,16 @@
     heads_here = lw // HD
     row_count = own_count * count
     group = fsdp * ctx
-    score_scale = HD ** (-0.5)
     piece = qkv_weight.shape[1]
     packed = jnp.concatenate(
-        [qkv_weight[0], qkv_weight[1], qkv_weight[2], out_weight.T, up_weight, down_weight.T],
-        axis=1,
+        [qkv_weight[0], qkv_weight[1], qkv_weight[2], out_weight.T, up_weight], axis=1
     )
     packed, full_in = comm[0](packed, block_input, count)
     packed = packed.reshape(width, packed.shape[2])
     full_in = full_in.reshape(row_count, width)
     qkv_full = packed[:, : 3 * lw]
     out_t = packed[:, 3 * lw : 4 * lw]
-    up_full = packed[:, 4 * lw : 4 * lw + hidden]
-    down_t = packed[:, 4 * lw + hidden :]
+    up_full = packed[:, 4 * lw :]
     gain_one = norm1_gain.astype(wide)
     gain_two = norm2_gain.astype(wide)
     normed, inv_std = normalize(full_in.astype(wide))
@@ -563,16 +728,14 @@
     keys_values = jnp.concatenate(
         [keys_here.reshape(row_count, lw), projected[:, 2 * lw :].astype(narrow)], axis=1
     )
-    full_cot, keys_values = comm[1](cotangent, keys_values, count)
+    queries = queries.reshape(row_count, lw)
+    starts = doc_start.reshape(row_count, 1)
+    down_t, full_cot, keys_values, attended = comm[1](
+        down_weight.T, cotangent, keys_values, queries, starts, count
+    )
+    down_t = down_t.reshape(width, hidden)
     full_cot = full_cot.reshape(row_count, width)
-    length = ctx * row_count
-    keys_values = keys_values.reshape(length, 2 * lw)
-    keys_all = keys_values[:, :lw].reshape(length, heads_here, HD)
-    values_all = keys_values[:, lw:].reshape(length, heads_here, HD)
-    attn_probs = attention_probs(queries, keys_all, query_pos, doc_start)
-    probs_b = attn_probs.astype(narrow)
-    attended = jnp.einsum("hqk,khd->qhd", probs_b, values_all, preferred_element_type=wide)
-    attended = attended.reshape(row_count, lw).astype(narrow)
+    keys_values = keys_values.reshape(ctx * row_count, 2 * lw)
     pre_act = dot(second_in, up_full) + up_bias.astype(wide)
     activated, gelu_slope = gelu_parts(pre_act)
     act_b = activated.astype(narrow)
@@ -584,34 +747,24 @@
     grad_up_local = dot(second_in, d_pre, rows)
     grad_down_local = dot(full_cot, act_b, rows)
     up_bias_grad = jnp.sum(d_pre.astype(wide), axis=0)
-    d_heads = d_attended.reshape(row_count, heads_here, HD)
-    d_values = jnp.einsum("hqk,qhd->khd", probs_b, d_heads, preferred_element_type=wide)
-    d_probs = jnp.einsum("qhd,khd->hqk", d_heads, values_all, preferred_element_type=wide)
-    delta_sum = jnp.sum(attn_probs * d_probs, axis=2, keepdims=True)
-    d_scores = (attn_probs * (d_probs - delta_sum)).astype(narrow)
-    d_query = (
-        jnp.einsum("hqk,khd->qhd", d_scores, keys_all, preferred_element_type=wide) * score_scale
-    )
-    d_keys = (
-        jnp.einsum("hqk,qhd->khd", d_scores, queries, preferred_element_type=wide) * score_scale
-    )
-    key_grads = jnp.concatenate([d_keys.reshape(length, lw), d_values.reshape(length, lw)], axis=1)
-    key_grads = key_grads.reshape(ctx, row_count, 2 * lw)
-    mlp_grads, summed, key_far = comm[2](
+    mlp_grads, summed, d_query, key_own = comm[2](
         jnp.concatenate([grad_up_local.astype(narrow), grad_down_local.astype(narrow)], axis=1)
         .reshape(group, piece, 2 * hidden),
         forward.astype(narrow).reshape(count, own_count, width),
-        key_grads.astype(narrow),
+        queries,
+        keys_values,
+        d_attended,
+        starts,
         count,
     )
     block_output = (
         block_input.astype(wide) + summed + out_bias.astype(wide) + down_bias.astype(wide)
     ).astype(narrow)
-    key_own = lax.dynamic_index_in_dim(key_grads, lax.axis_index("ctx"), 0, keepdims=False)
-    key_own = key_own + key_far.astype(wide)
     d_qkv = jnp.concatenate(
         [
-            rotate(d_query, cosine, -sine_table).reshape(row_count, lw),
+            rotate(
+                d_query.reshape(row_count, heads_here, HD), cosine, -sine_table
+            ).reshape(row_count, lw),
             rotate(
                 key_own[:, :lw].reshape(row_count, heads_here, HD), cosine, -sine_table
             ).reshape(row_count, lw),

time: 164 us -> 174 us (1.061)
  Pallas kernels: 85 us -> 112 us
  matrix products: 42.2 us -> 17.1 us
  local copies, waits for them, and re-layouts: 24.6 us -> 32.9 us
    pallas_call x4, Pallas kernels: 85 us -> 112 us  [call(): pl.pallas_call(body, out_shape=outs, in_specs=[VMEM] * len(inputs), out_s...]
    dot_general x5 -> x0, matrix products: 14.8 us -> none  [the longest x1 3.92 us: local(): jnp.einsum('hqk,khd->qhd', probs_b, values_all, preferred_element_type=wide)]
    sub x1 -> x0, matrix products: 6.88 us -> none  [attention_probs(): exponent = jnp.where(allowed[None], jnp.exp(masked - row_peak), 0.0)]
    unnamed x106 -> x80, local copies, waits for them, and re-layouts: 9.45 us -> 13.9 us
    concatenate x4 -> x0, local copies, waits for them, and re-layouts: 4.09 us -> none  [local(): jnp.concatenate([d_keys.reshape(length, lw), d_values.reshape(length, lw)...]
    dot_general x12, matrix products: 20.5 us -> 17.1 us  [dot(): lax.dot_general(a, b, (dims, ((), ())), preferred_element_type=jnp.float32)]
    slice x2, local copies, waits for them, and re-layouts: 0.21 us -> 2.06 us  [local(): key_own[:, :lw].reshape(row_count, heads_here, HD)]
where the time goes in v2:
time: 174 us; the launch traced here: 173 us
  Pallas kernels  112 us (64%)
  local copies, waits for them, and re-layouts  32.9 us (19%)
  matrix products  17.1 us (10%)
  other arithmetic  9.94 us (6%)
    pallas_call x4, Pallas kernels, call(): pl.pallas_call(body, out_shape=outs, in_specs=[VMEM] * len(inputs), out_s...  112 us
    dot_general x12, matrix products, dot(): lax.dot_general(a, b, (dims, ((), ())), preferred_element_type=jnp.float32)  17.1 us
    unnamed x80, local copies, waits for them, and re-layouts  13.9 us
    concatenate x1, local copies, waits for them, and re-layouts, local(): jnp.concatenate([grad_up_local.astype(narrow), grad_down_local.astype(nar...  4.26 us

profile of v2, /device:TPU:0, one launch (start us, length us, event | category | flops | bytes accessed | tf_op | source)
XLA Modules:
  0.0 173.1 jit_solution(15701855998825673987)
XLA Ops:
  2.5 1.0 concatenate.58.w
  4.4 20.5 %shard_map.254 = (bf16[8,96,1536]{2,1,0:T(8,128)(2,1)S(1)}, bf16[4,128,768]{2,1,0:T(8,128)(2,1)S(1)}) custom-call(bf16[96,1536]{1,0:T(8,128)(2,1)S(1)} %concatenate.58.w, bf16[128,768]{1,0:T(8,128)(2,1)S(1)} %copy-done), custom_call_target="tpu_custom_call" | custom-call | tf_op jit(solution)/shard_map/pallas_call | solution.py:452
  24.9 1.4 copy-done.12
  27.0 1.4 add_convert_fusion.3
  29.3 2.0 %convolution_add_fusion.1 = f32[512,576]{1,0:T(8,128)S(1)} fusion(bf16[512,768]{1,0:T(8,128)(2,1)S(1)} %get-tuple-element.100, bf16[768,1536]{1,0:T(8,128)(2,1)} %bitcast.72, f32[576]{0:T(1024)S(1)} %reshape.232), kind=kOutput, calls=%fused_computation.24 | convolution fusion | flops 453279744 | bytes 2951424 | tf_op jit(solution)/shard_map/dot_general | solution.py:670
  34.7 1.1 slice.237
  36.3 25.0 %shard_map.255 = (bf16[8,96,768]{2,1,0:T(8,128)(2,1)S(1)}, bf16[4,128,768]{2,1,0:T(8,128)(2,1)S(1)}, bf16[2,512,384]{2,1,0:T(8,128)(2,1)S(1)}, bf16[512,192]{1,0:T(8,128)(2,1)S(1)}) custom-call(bf16[96,768]{1,0:T(8,128)(2,1)S(1)} %bitcast.78, bf16[128,768]{1,0:T(8,128)(2,1)S(1)} %copy-done.2, bf16[512,384]{1,0:T(8,128)(2,1)S(1)} %pad_maximum_fusion.3.k, ...), custom_call_target="tpu_custom_call" | custom-call | tf_op jit(solution)/shard_map/pallas_call | solution.py:452
  61.3 1.8 %fusion.26 = f32[512,768]{1,0:T(8,128)S(1)} fusion(bf16[512,192]{1,0:T(8,128)(2,1)S(1)} %get-tuple-element.31, bf16[768,1536]{1,0:T(8,128)(2,1)} %bitcast.73), kind=kOutput, calls=%fused_computation.58 | convolution fusion | flops 150994944 | bytes 2162688 | tf_op jit(solution)/shard_map/dot_general | solution.py:670
  64.1 1.7 add_convert_fusion.1
  65.8 1.7 convert_reduce_fusion
  69.3 1.6 pad_maximum_fusion
  70.8 4.3 %copy.62 = bf16[768,1536]{1,0:T(8,128)(2,1)} copy(bf16[768,1536]{0,1:T(8,128)(2,1)} %pad_maximum_fusion) | data formatting | bytes 4718592 | tf_op jit(solution)/shard_map/concatenate | solution.py:751
  75.1 1.6 convolution_convert_fusion.4
  76.9 1.1 copy-done.4
  78.0 1.1 copy-done.5
  79.2 36.4 %shard_map.256 = (f32[96,1536]{1,0:T(8,128)S(1)}, f32[128,768]{1,0:T(8,128)S(1)}, f32[512,192]{1,0:T(8,128)S(1)}, f32[512,384]{1,0:T(8,128)S(1)}) custom-call(bf16[8,96,1536]{2,1,0:T(8,128)(2,1)} %bitcast.81, bf16[4,128,768]{2,1,0:T(8,128)(2,1)S(1)} %bitcast.70, bf16[512,192]{1,0:T(8,128)(2,1)S(1)} %copy.60.q, bf16[1024,384]{1,0:T(8,128)(2,1)S(1)} %bitcast.69, ...), custom_call_target="tpu_custom_call" | custom-call | tf_op jit(solution)/shard_map/pallas_call | solution.py:452
  118.8 1.2 copy.67
  124.8 1.3 slice.236
  126.8 2.2 %fusion.10 = f32[512,768]{1,0:T(8,128)S(1)} fusion(bf16[768,1536]{1,0:T(8,128)(2,1)} %bitcast.75, bf16[512,192]{1,0:T(8,128)(2,1)S(1)} %slice.236, bf16[512,192]{1,0:T(8,128)(2,1)S(1)} %copy.69, bf16[512,192]{1,0:T(8,128)(2,1)S(1)} %copy.68), kind=kOutput, calls=%fused_computation.33 | convolution fusion | flops 454754304 | bytes 3145728 | tf_op jit(solution)/shard_map/dot_general | solution.py:670
  129.0 1.1 fusion.40
  130.3 2.1 %convolution_convert_fusion.2 = bf16[768,576]{0,1:T(8,128)(2,1)S(1)} fusion(bf16[512,768]{1,0:T(8,128)(2,1)} %copy-done.20, bf16[512,192]{1,0:T(8,128)(2,1)} %copy-done.19, bf16[512,192]{1,0:T(8,128)(2,1)} %copy-done.18, bf16[512,192]{1,0:T(8,128)(2,1)} %copy-done.17), kind=kOutput, calls=%fused_computation.23 | convolution fusion | flops 455196672 | bytes 2260992 | tf_op jit(solution)/shard_map/dot_general | solution.py:670
  132.9 1.1 pad_maximum_fusion.1
  134.0 1.6 copy.70
  135.5 29.7 %shard_map.257 = (f32[96,768]{1,0:T(8,128)S(1)}, f32[128,768]{1,0:T(8,128)S(1)}, f32[8,768]{1,0:T(8,128)S(1)}) custom-call(bf16[8,96,768]{2,1,0:T(8,128)(2,1)S(1)} %bitcast.64, bf16[4,128,768]{2,1,0:T(8,128)(2,1)S(1)} %bitcast.71, f32[8,768]{1,0:T(8,128)S(1)} %stack.35.m), custom_call_target="tpu_custom_call" | custom-call | tf_op jit(solution)/shard_map/pallas_call | solution.py:452
  (150 shorter events, 27.5 us)
Async XLA Ops:
  0.6 26.3 %copy-start.28 = (bf16[768]{0:T(1024)(128)(2,1)S(1)}, bf16[768]{0:T(1024)(128)(2,1)}, u32[]{:S(2)}) copy-start(bf16[768]{0:T(1024)(128)(2,1)} %param.20) | copy-start | bytes 4612
  0.7 26.3 %copy-start.29 = (bf16[768]{0:T(1024)(128)(2,1)S(1)}, bf16[768]{0:T(1024)(128)(2,1)}, u32[]{:S(2)}) copy-start(bf16[768]{0:T(1024)(128)(2,1)} %param.18) | copy-start | bytes 4612
  0.7 26.3 %copy-start.30 = (bf16[768]{0:T(1024)(128)(2,1)S(1)}, bf16[768]{0:T(1024)(128)(2,1)}, u32[]{:S(2)}) copy-start(bf16[768]{0:T(1024)(128)(2,1)} %param.21) | copy-start | bytes 4612
  0.7 26.3 %copy-start.31 = (bf16[768]{0:T(1024)(128)(2,1)S(1)}, bf16[768]{0:T(1024)(128)(2,1)}, u32[]{:S(2)}) copy-start(bf16[768]{0:T(1024)(128)(2,1)} %param.19) | copy-start | bytes 4612
  24.9 1.4 copy-start.12
  26.5 1.9 %copy-start.32 = (bf16[3,192]{1,0:T(4,128)(2,1)S(1)}, bf16[3,192]{1,0:T(4,128)(2,1)}, u32[]{:S(2)}) copy-start(bf16[3,192]{1,0:T(4,128)(2,1)} %param.23) | copy-start | bytes 3460
  26.9 4.4 %copy-start.25 = (f32[512]{0:T(512)}, f32[512]{0:T(512)S(1)}, u32[]{:S(2)}) copy-start(f32[512]{0:T(512)S(1)} %rsqrt_bitcast_fusion) | copy-start | bytes 6148
  34.5 1.7 copy-start.2
  34.5 1.7 copy-start.15
  36.2 26.9 %copy-start.33 = (bf16[768]{0:T(1024)(128)(2,1)S(1)}, bf16[768]{0:T(1024)(128)(2,1)}, u32[]{:S(2)}) copy-start(bf16[768]{0:T(1024)(128)(2,1)} %param.27) | copy-start | bytes 4612
  36.3 26.9 %copy-start.13 = (bf16[8,96,1536]{2,1,0:T(8,128)(2,1)S(1)}, bf16[8,96,1536]{2,1,0:T(8,128)(2,1)}, u32[]{:S(2)}) copy-start(bf16[8,96,1536]{2,1,0:T(8,128)(2,1)} %copy-done.12) | copy-start | bytes 7077892
  36.3 26.9 %copy-start.21 = (bf16[512,768]{1,0:T(8,128)(2,1)S(1)}, bf16[512,768]{1,0:T(8,128)(2,1)}, u32[]{:S(2)}) copy-start(bf16[512,768]{1,0:T(8,128)(2,1)} %get-tuple-element.99) | copy-start | bytes 2359300
  61.3 2.8 %copy-start.3 = (bf16[2,512,384]{2,1,0:T(8,128)(2,1)}, bf16[2,512,384]{2,1,0:T(8,128)(2,1)S(1)}, u32[]{:S(2)}) copy-start(bf16[2,512,384]{2,1,0:T(8,128)(2,1)S(1)} %get-tuple-element.32) | copy-start | bytes 2359300
  118.0 2.7 %copy-start.8 = (f32[512,192]{1,0:T(8,128)S(1)}, f32[512,192]{1,0:T(8,128)}, u32[]{:S(2)}) copy-start(f32[512,192]{1,0:T(8,128)} %copy-done.7) | copy-start | bytes 1179652
  124.6 1.8 %copy-start.17 = (bf16[512,192]{1,0:T(8,128)(2,1)}, bf16[512,192]{1,0:T(8,128)(2,1)S(1)}, u32[]{:S(2)}) copy-start(bf16[512,192]{1,0:T(8,128)(2,1)S(1)} %copy.68) | copy-start | bytes 589828
  124.8 1.6 copy-start.18
  126.8 2.2 %copy-start.14 = (bf16[8,96,1536]{2,1,0:T(8,128)(2,1)S(1)}, bf16[8,96,1536]{2,1,0:T(8,128)(2,1)}, u32[]{:S(2)}) copy-start(bf16[8,96,1536]{2,1,0:T(8,128)(2,1)} %copy-done.12) | copy-start | bytes 7077892
  126.8 2.2 %copy-start.26 = (f32[512]{0:T(512)S(1)}, f32[512]{0:T(512)}, u32[]{:S(2)}) copy-start(f32[512]{0:T(512)} %copy-done.25) | copy-start | bytes 6148
  126.8 2.2 %copy-start.37 = (bf16[512,768]{1,0:T(8,128)(2,1)S(1)}, bf16[512,768]{1,0:T(8,128)(2,1)}, u32[]{:S(2)}) copy-start(bf16[512,768]{1,0:T(8,128)(2,1)} %copy-done.36) | copy-start | bytes 2359300
  135.5 31.5 %copy-start.1 = (bf16[128,768]{1,0:T(8,128)(2,1)S(1)}, bf16[128,768]{1,0:T(8,128)(2,1)}, u32[]{:S(2)}) copy-start(bf16[128,768]{1,0:T(8,128)(2,1)} %r.2) | copy-start | bytes 589828
  165.3 2.3 %copy-start.34 = (bf16[768]{0:T(1024)(128)(2,1)S(1)}, bf16[768]{0:T(1024)(128)(2,1)}, u32[]{:S(2)}) copy-start(bf16[768]{0:T(1024)(128)(2,1)} %param.25) | copy-start | bytes 4612
  165.3 2.3 %copy-start.35 = (bf16[768]{0:T(1024)(128)(2,1)S(1)}, bf16[768]{0:T(1024)(128)(2,1)}, u32[]{:S(2)}) copy-start(bf16[768]{0:T(1024)(128)(2,1)} %param.29) | copy-start | bytes 4612
  165.3 2.4 %copy-start.11 = (f32[128,768]{1,0:T(8,128)S(1)}, f32[128,768]{1,0:T(8,128)}, u32[]{:S(2)}) copy-start(f32[128,768]{1,0:T(8,128)} %copy-done.10) | copy-start | bytes 1179652
  170.9 2.1 %copy-start.23 = (f32[768]{0:T(1024)}, f32[768]{0:T(1024)S(1)}, u32[]{:S(2)}) copy-start(f32[768]{0:T(1024)S(1)} %get-tuple-element.154) | copy-start | bytes 9220
  (14 other events, 12.4 us)
